TPU v7x, 32 devices: a whole 2x2x4 slice. The times are simulated.
32 devices in a mesh: fsdp: 16 (over z, y, core), seq: 2 (over x).
Axes of the slice: x: 2, y: 2, z: 4, core: 2. Of those that a mesh axis runs over, the one named last changes fastest.
Arguments:
- stream: bfloat16 [6144, 1024], P(('fsdp', 'seq')), may hold values from -6 to 6
- cotangent: bfloat16 [6144, 1024], P(('fsdp', 'seq')), may hold values from -6 to 6
- doc_lengths: int32 [10], replicated, may hold values from 1 to 1153, 6144 in all
- attention_gain: bfloat16 [1024], P('fsdp'), may hold values from 0.5 to 1.5
- query_weight: bfloat16 [1024, 1024], P('fsdp'), may hold values from -0.1875 to 0.1875
- key_matrix: bfloat16 [1024, 512], P('fsdp'), may hold values from -0.1875 to 0.1875
- value_matrix: bfloat16 [1024, 512], P('fsdp'), may hold values from -0.1875 to 0.1875
- query_gain: bfloat16 [64], P('fsdp'), may hold values from 0.5 to 1.5
- key_gain: bfloat16 [64], P('fsdp'), may hold values from 0.5 to 1.5
- output_weight: bfloat16 [1024, 1024], P('fsdp'), may hold values from -3 to 3
- feedforward_gain: bfloat16 [1024], P('fsdp'), may hold values from 0.5 to 1.5
- gate_weight: bfloat16 [1024, 4608], P('fsdp'), may hold values from -0.1875 to 0.1875
- up_weight: bfloat16 [1024, 4608], P('fsdp'), may hold values from -0.1875 to 0.1875
- down_weight: bfloat16 [4608, 1024], P('fsdp'), may hold values from -0.09375 to 0.09375
Outputs:
- result: bfloat16 [6144, 1024], P(('fsdp', 'seq'))
- grad_stream: bfloat16 [6144, 1024], P(('fsdp', 'seq'))
- grad_attention_gain: float32 [1024], P('fsdp')
- grad_query: float32 [1024, 1024], P('fsdp')
- grad_key: float32 [1024, 512], P('fsdp')
- grad_value: float32 [1024, 512], P('fsdp')
- grad_query_gain: float32 [64], P('fsdp')
- grad_key_gain: float32 [64], P('fsdp')
- grad_output: float32 [1024, 1024], P('fsdp')
- grad_feedforward_gain: float32 [1024], P('fsdp')
- grad_gate: float32 [1024, 4608], P('fsdp')
- grad_up: float32 [1024, 4608], P('fsdp')
- grad_down: float32 [4608, 1024], P('fsdp')
Inputs may be any that keep to these rules, and one draw needn't show every extreme that they name: `doc_lengths`: they sum to 6144, and the longest has exactly 1153 tokens.
All inputs are finite; a program needn't handle non-finite values.
Results may differ from a plain program's by a relative error of at most 0.03.
Values may be sent and summed in bfloat16 or wider, within the bound.
No kernel may reach another device: no remote copies, remote signals or barrier semaphores. Data moves between devices by JAX's collectives and lax.ppermute only.
A program may use at most 192 MiB of HBM per device.

v0:
```python
import functools

import jax
import jax.numpy as jnp
from jax import lax
from jax.experimental import pallas as pl
from jax.experimental.pallas import tpu as pltpu
from jax.sharding import Mesh, PartitionSpec as P

QUERY_HEAD_COUNT = 16
KEY_VALUE_HEADS = 8
HEAD_SIZE = 64
DOC_MIN = 1024
EPS = 1e-05
THETA = 1000000.0
GROUP = 8
BF16 = jnp.bfloat16
F32 = jnp.float32
VMEM_LIMIT = 60 * 1024 * 1024

VM = pl.BlockSpec(memory_space=pltpu.VMEM)
SM = pl.BlockSpec(memory_space=pltpu.SMEM)
FAR = pl.BlockSpec(memory_space=pl.ANY)


def nn(left, right):
    return lax.dot_general(left, right, (((1,), (0,)), ((), ())), preferred_element_type=F32)


def nt(left, right):
    return lax.dot_general(left, right, (((1,), (1,)), ((), ())), preferred_element_type=F32)


def tn(left, right):
    return lax.dot_general(left, right, (((0,), (0,)), ((), ())), preferred_element_type=F32)


def call(kernel, outs, n_smem, args, flops, name, scratch=(), far_in=(), far_out=()):
    bytes_moved = sum(a.size * a.dtype.itemsize for a in args) + sum(
        o.size * o.dtype.itemsize for o in outs
    )
    return pl.pallas_call(
        kernel,
        out_shape=outs,
        in_specs=[
            SM if n < n_smem else FAR if n in far_in else VM for n in range(len(args))
        ],
        out_specs=[FAR if n in far_out else VM for n in range(len(outs))],
        scratch_shapes=list(scratch),
        compiler_params=pltpu.CompilerParams(vmem_limit_bytes=VMEM_LIMIT),
        cost_estimate=pl.CostEstimate(flops=flops, bytes_accessed=bytes_moved, transcendentals=0),
        name=name,
    )(*args)


def shape(dims, dtype):
    return jax.ShapeDtypeStruct(dims, dtype)


def rotated(x, lane):
    return jnp.where(lane % 64 < 32, -pltpu.roll(x, 96, 1), pltpu.roll(x, 32, 1))


def head_sum(x, low):
    first = jnp.sum(jnp.where(low, x, 0.0), axis=1, keepdims=True)
    second = jnp.sum(jnp.where(low, 0.0, x), axis=1, keepdims=True)
    return jnp.where(low, first, second)


def pack_heads_kernel(kv_head, seq, meta, gains, q_ref, k_ref, v_ref, scale_ref, out_ref):
    count, rows = out_ref.shape[0], q_ref.shape[0]
    per = gains.shape[0] // 2
    scale = scale_ref[...]
    lane = lax.broadcasted_iota(jnp.int32, (16, 256), 1)
    row = lax.broadcasted_iota(jnp.int32, (16, 256), 0)
    extra = jnp.zeros((16, 256), F32)
    for j in range(per):
        spot = (lane % 64 == meta[2] * per + j) & (row == 0)
        extra = jnp.where(spot & (lane < 128), gains[j], extra)
        extra = jnp.where(spot & (lane >= 128) & (lane < 192), gains[per + j], extra)
    extra = extra.astype(BF16)
    for s_at in range(seq):

        @pl.when(meta[3] == s_at)
        def _():
            for i_at in range(count):
                t = kv_head(i_at, s_at)
                out_ref[i_at, :rows, :128] = (
                    q_ref[:, 128 * t : 128 * t + 128].astype(F32) * scale
                ).astype(BF16)
                pair = 128 * (t // 2)
                key = k_ref[:, pair : pair + 128].astype(F32) * scale
                value = v_ref[:, pair : pair + 128].astype(F32) * scale
                if t % 2:
                    key = pltpu.roll(key, 64, 1)
                else:
                    value = pltpu.roll(value, 64, 1)
                low = lax.broadcasted_iota(jnp.int32, key.shape, 1) < 64
                out_ref[i_at, :rows, 128:] = jnp.where(low, key, value).astype(BF16)

    for i_at in range(count):
        out_ref[i_at, rows:, :] = extra


def send_heads_kernel(kv_head, seq, meta, gains, q_ref, k_ref, v_ref, scale_ref, *refs):
    *outs, heads = refs
    pack_heads_kernel(kv_head, seq, meta, gains, q_ref, k_ref, v_ref, scale_ref, heads)
    for m, out in enumerate(outs):
        out[...] = heads[meta[4] ^ m]


def send_wide_kernel(seq, outer, meta, gate_ref, up_ref, scale_ref, *refs):
    *outs, packed, wide = refs
    count = len(outs)
    piece = gate_ref.shape[1] // (outer * count * seq)
    local = outer * piece
    main = local - 64
    scale = scale_ref[...]
    for s_at in range(seq):

        @pl.when(meta[3] == s_at)
        def _():
            for i_at in range(count):
                for side, source in enumerate((gate_ref, up_ref)):
                    for o_at in range(outer):
                        at = ((o_at * count + i_at) * seq + s_at) * piece
                        wide[side, :, o_at * piece : (o_at + 1) * piece] = (
                            source[:, at : at + piece].astype(F32) * scale
                        )
                packed[i_at, :, :main] = wide[0, :, :main].astype(BF16)
                packed[i_at, :, main : main + 128] = jnp.concatenate(
                    [wide[0, :, main:], wide[1, :, main:]], axis=1
                ).astype(BF16)
                packed[i_at, :, main + 128 :] = wide[1, :, :main].astype(BF16)

    for m, out in enumerate(outs):
        out[...] = packed[meta[4] ^ m]


def unpack_wide_kernel(outer, got_ref, gate_w, up_w, scale_ref, gate_ref, up_ref, gain_ref):
    ranks, rows = got_ref.shape[0], got_ref.shape[1]
    local = got_ref.shape[2] // 2
    piece, main = local // outer, local - 64
    for rank in range(ranks):
        got = got_ref[rank].astype(F32)
        up = jnp.concatenate([got[:, local + 64 :], got[:, local : local + 64]], axis=1)
        for value, out in ((got[:, :local], gate_ref), (up, up_ref)):
            for o_at in range(outer):
                at = (o_at * ranks + rank) * piece
                out[:, at : at + piece] = value[:, o_at * piece : (o_at + 1) * piece]
    scale = scale_ref[...]
    total = jnp.zeros((rows, 1), F32)
    for weight, out in ((gate_w, gate_ref), (up_w, up_ref)):
        raw = out[...]
        total = total + jnp.sum(raw * weight[...].astype(F32), axis=1, keepdims=True)
        out[...] = raw * scale
    gain_ref[...] = jnp.broadcast_to(total, gain_ref.shape)


def owners_kernel(
    kv_head, seq, per, meta, got_ref, q_w, k_w, v_w, scale_ref, q_ref, k_ref, v_ref, gain_ref, head_ref
):
    ranks, rows = got_ref.shape[0], q_w.shape[0]
    scale = scale_ref[...]
    total = jnp.zeros((rows, 1), F32)
    sums = jnp.zeros((16, 256), F32)
    low = lax.broadcasted_iota(jnp.int32, (rows, 128), 1) < 64
    back = {}
    for rank in range(ranks):
        t = kv_head(rank // seq, rank % seq)
        there = slice(128 * t, 128 * t + 128)
        part = got_ref[rank, :rows, :128].astype(F32)
        total = total + jnp.sum(part * q_w[:, there].astype(F32), axis=1, keepdims=True)
        q_ref[:, there] = part * scale
        back[t] = got_ref[rank, :rows, 128:].astype(F32)
        sums = sums + got_ref[rank, rows:, :].astype(F32)
    for t in range(0, ranks, 2):
        there = slice(64 * t, 64 * t + 128)
        key = jnp.where(low, back[t], pltpu.roll(back[t + 1], 64, 1))
        value = jnp.where(low, pltpu.roll(back[t], 64, 1), back[t + 1])
        for part, weight, out in ((key, k_w, k_ref), (value, v_w, v_ref)):
            total = total + jnp.sum(part * weight[:, there].astype(F32), axis=1, keepdims=True)
            out[:, there] = part * scale
    gain_ref[...] = jnp.broadcast_to(total, gain_ref.shape)
    row = sums[0:1, :128]
    row = row + pltpu.roll(row, 64, 1)
    row = jnp.concatenate([row, sums[0:1, 128:]], axis=1)
    lane = lax.broadcasted_iota(jnp.int32, (8, 128), 1)
    out = jnp.zeros((8, 128), F32)
    for j in range(per):
        here = lax.broadcasted_iota(jnp.int32, (1, 256), 1) % 128 == meta[2] * per + j
        picked = jnp.where(here, row, 0.0)
        q_j = jnp.sum(picked[:, :128], axis=1, keepdims=True)
        k_j = jnp.sum(picked[:, 128:], axis=1, keepdims=True)
        out = jnp.where(lane == j, q_j, out)
        out = jnp.where(lane == 64 + j, k_j, out)
    head_ref[...] = out


def prepare_kernel(meta, *refs):
    blocks, refs = refs[:GROUP], refs[GROUP:]
    sources = refs[:-10]
    cos_ref, sin_ref, q_ref, kv_ref, tail_ref, lin_ref, all_ref, w_ref, gain_ref, sems = refs[-10:]
    rows = all_ref.shape[0] // GROUP
    copies = block_copies(blocks, [all_ref.at[pl.ds(k * rows, rows)] for k in range(GROUP)], sems)
    for copy in copies:
        copy.start()
    gains = jnp.zeros((1, 256), F32)
    for m, source in enumerate(sources):
        parts, k_rows = source.shape[0], source.shape[1] - 16
        at = pl.multiple_of((meta[5] ^ m) * (parts * k_rows), parts * k_rows & -(parts * k_rows))
        if len(sources) == 1:
            at = 0
        w_ref[pl.ds(at, parts * k_rows), :] = source[:, :k_rows, :].reshape(parts * k_rows, 256)
        gains = gains + jnp.sum(source[:, k_rows:, :].astype(F32), axis=0)[0:1]
    gain_ref[...] = jnp.broadcast_to(gains, gain_ref.shape)
    weights = w_ref[...]
    lane = lax.broadcasted_iota(jnp.int32, (rows, 128), 1)
    low = lane < 64

    @pl.loop(0, GROUP)
    def _(k):
        at = pl.ds(pl.multiple_of((meta[0] ^ k) * rows, rows & -rows), rows)
        at_step(k, copies, lambda copy: copy.wait())
        lin = nn(all_ref[pl.ds(pl.multiple_of(k * rows, rows & -rows), rows), :], weights)
        lin_ref[at, :] = lin
        cosine, sine = cos_ref[at, :], sin_ref[at, :]
        front, back = lin[:, :128], lin[:, 128:]
        head = front * lax.rsqrt(head_sum(front * front, low) * (1 / 64) + EPS) * gains[:, :128]
        head = (head * cosine + rotated(head, lane) * sine) * (HEAD_SIZE**-0.5)
        q_ref[0, at, :] = jnp.where(low, head, 0.0).astype(BF16)
        q_ref[1, at, :] = jnp.where(low, pltpu.roll(head, 64, 1), 0.0).astype(BF16)
        key = back * lax.rsqrt(head_sum(back * back, low) * (1 / 64) + EPS) * gains[:, 128:]
        key = key * cosine + rotated(key, lane) * sine
        kv_ref[at, :] = jnp.where(low, key, back).astype(BF16)
    tail_ref[...] = kv_ref[kv_ref.shape[0] - tail_ref.shape[0] :, :]


def query_bounds(lengths, first, count):
    lane = lax.broadcasted_iota(jnp.int32, (1, 2 * count), 1)
    place = first + jnp.where(lane >= count, lane - count, lane)
    start = jnp.zeros((1, 2 * count), jnp.int32)
    begin, lowest = jnp.int32(0), jnp.int32(0)
    for d in range(lengths.shape[0]):
        start = jnp.where(place >= begin, begin, start)
        lowest = jnp.where(first >= begin, begin, lowest)
        begin = begin + lengths[d]
    return place, start, lowest


def fill_keys(parts, keys_ref):
    @pl.when(pl.program_id(0) == 0)
    def _():
        at = 0
        for part in parts:
            keys_ref[at : at + part.shape[0], :] = part[...]
            at += part.shape[0]


def attend_kernel(halo, span, meta, lengths, q_ref, *refs):
    *parts, out_ref, log_ref, kv_ref = refs
    step = pl.program_id(0)
    base = meta[1] - halo
    fill_keys(parts, kv_ref)
    place, start, lowest = query_bounds(lengths, meta[1] + step * span, span)
    queries = q_ref[...].reshape(2 * span, 128)
    iota = lax.broadcasted_iota(jnp.int32, (span, 2 * span), 0)
    first = jnp.maximum(lowest - base, 0) // span

    def body(at, carry):
        total, mixed = carry
        offset = pl.multiple_of(at * span, span)
        keys = kv_ref[pl.ds(offset, span), :]
        score = nt(keys, queries)
        moved = base + offset
        weight = jnp.where((iota >= start - moved) & (iota <= place - moved), jnp.exp(score), 0.0)
        total = total + jnp.sum(weight, axis=0, keepdims=True)
        mixed = mixed + tn(keys, weight.astype(BF16))
        return total, mixed

    total, mixed = lax.fori_loop(
        first,
        step + halo // span + 1,
        body,
        (jnp.zeros((1, 2 * span), F32), jnp.zeros((128, 2 * span), F32)),
    )
    mixed = mixed * (1.0 / total)
    side = jnp.concatenate([mixed[64:, :span], mixed[64:, span:]], axis=0)
    out_ref[...] = side.T.astype(BF16)
    log_ref[...] = jnp.broadcast_to(jnp.log(total), (8, 2 * span))


def attend_back_kernel(halo, span, meta, lengths, q_ref, *refs):
    *parts, grad_ref, out_ref, log_ref, dq_ref, early_ref, own_ref, kv_ref, dkv_ref = refs
    step = pl.program_id(0)
    base = meta[1] - halo
    fill_keys(parts, kv_ref)

    @pl.when(step == 0)
    def _():
        dkv_ref[...] = jnp.zeros_like(dkv_ref)

    place, start, lowest = query_bounds(lengths, meta[1] + step * span, span)
    queries = q_ref[...].reshape(2 * span, 128)
    grad = grad_ref[...].astype(F32)
    low = lax.broadcasted_iota(jnp.int32, (span, 128), 1) < 64
    grads = jnp.concatenate(
        [jnp.where(low, 0.0, pltpu.roll(grad, 64, 1)), jnp.where(low, 0.0, grad)], axis=0
    ).astype(BF16)
    both = (grad * out_ref[...].astype(F32)).T
    row_sum = jnp.concatenate(
        [jnp.sum(both[:64], axis=0, keepdims=True), jnp.sum(both[64:], axis=0, keepdims=True)],
        axis=1,
    )
    logs = log_ref[0:1, :]
    iota = lax.broadcasted_iota(jnp.int32, (span, 2 * span), 0)
    first = jnp.maximum(lowest - base, 0) // span

    def body(at, dq):
        offset = pl.multiple_of(at * span, span)
        keys = kv_ref[pl.ds(offset, span), :]
        moved = base + offset
        weight = jnp.where(
            (iota >= start - moved) & (iota <= place - moved),
            jnp.exp(nt(keys, queries) - logs),
            0.0,
        )
        d_score = (weight * (nt(keys, grads) - row_sum)).astype(BF16)
        dkv_ref[pl.ds(offset, span), :] += nn(d_score, queries) + nn(weight.astype(BF16), grads)
        return dq + tn(keys, d_score)

    dq = lax.fori_loop(
        first, step + halo // span + 1, body, jnp.zeros((128, 2 * span), F32)
    ) * (HEAD_SIZE**-0.5)
    dq_ref[...] = jnp.concatenate([dq[:64, :span], dq[:64, span:]], axis=0).T.astype(BF16)

    @pl.when(step == pl.num_programs(0) - 1)
    def _():
        early_ref[...] = dkv_ref[:halo, :].astype(BF16)
        own_ref[...] = dkv_ref[halo:, :]


def block_copies(sources, targets, sems):
    return [pltpu.make_async_copy(*pair, sems.at[n]) for n, pair in enumerate(zip(sources, targets))]


def at_step(step, copies, act):
    for n, copy in enumerate(copies):

        @pl.when(step == n)
        def _():
            act(copy)


def project_kernel(meta, att_ref, w_ref, *refs):
    *outs, held, sems = refs
    rows = held.shape[1]
    copies = block_copies([held.at[k] for k in range(GROUP)], outs, sems)

    @pl.loop(0, GROUP)
    def _(k):
        at = pl.ds(pl.multiple_of((meta[0] ^ k) * rows, rows & -rows), rows)
        held[k] = nn(att_ref[at, :], w_ref[...]).astype(BF16)
        at_step(k, copies, lambda copy: copy.start())

    for copy in copies:
        copy.wait()


def unproject_kernel(meta, *refs):
    blocks, refs = refs[:GROUP], refs[GROUP:]
    unproject_body(meta, blocks, *refs)


def unproject_into_kernel(meta, *refs):
    blocks, refs = refs[:GROUP], refs[GROUP:]
    w_ref, att_ref, _, out_ref, rest_ref, grad_ref, spot_ref, sem, held, sems = refs
    unproject_body(meta, blocks, w_ref, att_ref, out_ref, grad_ref, held, sems)
    o_rows = spot_ref.shape[2]
    spot_ref[...] = jnp.zeros_like(spot_ref)
    for n in range(2):
        spot_ref[2 * meta[3] + meta[4] % 2, n] = grad_ref[n * o_rows : (n + 1) * o_rows, :]
    copy = pltpu.make_async_copy(
        spot_ref, rest_ref.at[:, :, pl.ds(rest_ref.shape[2] - o_rows, o_rows)], sem
    )
    copy.start()
    copy.wait()


def unproject_body(meta, blocks, w_ref, att_ref, out_ref, grad_ref, held, sems):
    rows = held.shape[1]
    copies = block_copies(blocks, [held.at[k] for k in range(GROUP)], sems)
    for copy in copies:
        copy.start()

    def body(k, total):
        at_step(k, copies, lambda copy: copy.wait())
        at = pl.ds(pl.multiple_of((meta[0] ^ k) * rows, rows & -rows), rows)
        own = held[k]
        out_ref[at, :] = nt(own, w_ref[...]).astype(BF16)
        return total + tn(att_ref[at, :], own)

    grad_ref[...] = lax.fori_loop(
        0, GROUP, body, jnp.zeros(grad_ref.shape, F32)
    ).astype(BF16)


def finish_kernel(meta, dq_ref, own_ref, *refs):
    *backs, lin_ref, cos_ref, sin_ref, w_ref, gains_ref = refs[: -GROUP - 6]
    hidden = refs[-GROUP - 6 : -6]
    dlin_ref, gain_ref, dkv_ref, held_ref, hidden_held, sems = refs[-6:]
    dkv_ref[...] = own_ref[...]
    for back in backs:
        dkv_ref[dkv_ref.shape[0] - back.shape[0] :, :] += back[...].astype(F32)
    weights, gains = w_ref[...], gains_ref[0:1, :]
    rows = hidden_held.shape[1]
    lane = lax.broadcasted_iota(jnp.int32, (rows, 128), 1)
    low = lane < 64

    def body(block, gain_sums):
        at = pl.ds(pl.multiple_of(block * rows, rows & -rows), rows)
        cosine, sine = cos_ref[at, :], sin_ref[at, :]
        parts, sums = [], []
        for side, source in enumerate((dq_ref, dkv_ref)):
            lin = lin_ref[at, 128 * side : 128 * side + 128]
            factor = lax.rsqrt(head_sum(lin * lin, low) * (1 / 64) + EPS)
            plain = lin * factor
            given = source[at, :].astype(BF16).astype(F32)
            turned = given * cosine - rotated(given, lane) * sine
            sums.append(gain_sums[side] + jnp.sum(turned * plain, axis=0, keepdims=True))
            scaled = turned * gains[:, 128 * side : 128 * side + 128]
            grad = factor * (scaled - plain * (head_sum(scaled * plain, low) * (1 / 64)))
            parts.append(jnp.where(low, grad, given) if side else grad)
        held_ref[at, :] = jnp.concatenate(parts, axis=1).astype(BF16)
        return tuple(sums)

    gain_sums = lax.fori_loop(0, GROUP, body, (jnp.zeros((1, 128), F32),) * 2)
    copies = block_copies([hidden_held.at[k] for k in range(GROUP)], hidden, sems)

    @pl.loop(0, GROUP)
    def _(k):
        dlin = held_ref[pl.ds(pl.multiple_of((meta[0] ^ k) * rows, rows & -rows), rows), :]
        dlin_ref[pl.ds(pl.multiple_of(k * rows, rows & -rows), rows), :] = dlin
        hidden_held[k] = nt(dlin, weights).astype(BF16)
        at_step(k, copies, lambda copy: copy.start())

    for copy in copies:
        copy.wait()
    gain_ref[...] = jnp.broadcast_to(jnp.concatenate(gain_sums, axis=1), gain_ref.shape)


def project_grad_kernel(meta, n_ref, d_ref, gain_ref, *refs):
    *outs, grad_ref = refs
    parts, rows = outs[0].shape[0], outs[0].shape[1] - 16
    grad_ref[...] = tn(n_ref[...], d_ref[...]).astype(BF16)
    extra = jnp.where(
        lax.broadcasted_iota(jnp.int32, (16, 256), 0) == 0, gain_ref[0:1, :], 0.0
    ).astype(BF16)
    for m, out in enumerate(outs):
        first = (meta[5] ^ m) * (parts * rows) if len(outs) > 1 else 0
        for part in range(parts):
            at = first + part * rows
            if len(outs) > 1:
                at = pl.multiple_of(at, rows)
            out[part, :rows, :] = grad_ref[pl.ds(at, rows), :]
            out[part, rows:, :] = extra


def spread_sum_kernel(seq, *refs):
    *parts, out_ref = refs
    for i_at in range(parts[0].shape[0]):
        total = parts[0][i_at].astype(F32)
        for part in parts[1:]:
            total = total + part[i_at].astype(F32)
        total = total.astype(BF16)
        for s_at in range(seq):
            out_ref[i_at * seq + s_at] = total


def arrange_heads_kernel(meta, *refs):
    *pieces, out_ref = refs
    for m, piece in enumerate(pieces):
        for o_at in range(out_ref.shape[0]):
            out_ref[o_at, meta[4] ^ m] = piece[...]


def arrange_wide_kernel(meta, *refs):
    *pieces, out_ref = refs
    for m, piece in enumerate(pieces):
        out_ref[meta[4] ^ m] = piece[...]


def wide_grad_kernel(h_ref, d_ref, out_ref):
    chunk = out_ref.shape[2]

    @pl.loop(0, 2)
    def _(n):
        @pl.loop(0, out_ref.shape[0])
        def _(o_at):
            at = pl.ds(pl.multiple_of(o_at * chunk, chunk), chunk)
            out_ref[o_at, n] = tn(h_ref[:, at], d_ref[n]).astype(BF16)


def down_grad_kernel(rows, inner_ref, c_ref, out_ref):
    @pl.loop(0, 2)
    def _(n):
        grad = tn(inner_ref[n], c_ref[...]).astype(BF16)
        for o_at in range(out_ref.shape[0]):
            out_ref[o_at, n, :rows, :] = grad[o_at * rows : (o_at + 1) * rows]


def rest_out_kernel(meta, mine_ref, other_ref, down_ref, out_ref):
    rows = down_ref.shape[0] // 2
    mine, other = mine_ref[...].astype(F32), other_ref[...].astype(F32)
    out_ref[...] = mine[rows:] + other[rows:]
    first = meta[3] == 0
    down_ref[:rows, :] = jnp.where(first, mine[:rows], other[:rows])
    down_ref[rows:, :] = jnp.where(first, other[:rows], mine[:rows])


def near_kernel(*refs):
    for mine, far, out in zip(refs[:4], refs[4:8], refs[8:]):
        out[...] = (mine[...].astype(F32) + far[...].astype(F32)).astype(out.dtype)


def total_of(refs):
    total = refs[0][...].astype(F32)
    for ref in refs[1:]:
        total = total + ref[...].astype(F32)
    return total


def middle_kernel(*refs):
    *parts, middle_ref, plain_ref = refs
    middle = total_of(parts)
    middle_ref[...] = middle
    plain_ref[...] = normalized(middle)[0].astype(BF16)


def back_norm_kernel(*refs):
    source_ref, base_ref, *parts, full_ref, low_ref = refs
    plain, factor = normalized(source_ref[...].astype(F32))
    total = base_ref[...].astype(F32) + norm_back(total_of(parts), plain, factor)
    full_ref[...] = total
    low_ref[...] = total.astype(BF16)


def feed_kernel(count, down_rows, *refs):
    hs, cs, (wgu_in, wd_in), refs = refs[:count], refs[count : 2 * count], refs[2 * count :][:2], refs
    wgu_held, wd_held, total, sems = refs[-4:]
    fed_out, two_out = refs[-8 - 2 * count : -8 - count], refs[-8 - count : -8]
    h_ref, c_ref, dgu_ref, inner_ref = refs[-8:-4]
    up_rows = wgu_in.shape[2]

    def copies(part, n):
        source, target, step = (
            (wgu_in, wgu_held, up_rows),
            (wd_in, wd_held, down_rows),
        )[n]
        return [
            pltpu.make_async_copy(
                source.at[o_at, part, pl.ds(0, step)],
                target.at[part, pl.ds(o_at * step, step)],
                sems.at[2 * part + n, o_at],
            )
            for o_at in range(source.shape[0])
        ]

    for part in range(2):
        for n in range(2):
            for copy in copies(part, n):
                copy.start()
    deep = wd_held.shape[1]
    for part in range(2):
        wd_held[part, deep - 64 :, :] = jnp.zeros((64, wd_held.shape[2]), BF16)
    rows = hs[0].shape[0]
    hidden = jnp.concatenate([h[...] for h in hs], axis=0)
    cotangent = jnp.concatenate([c[...] for c in cs], axis=0)
    h_ref[...] = hidden
    c_ref[...] = cotangent
    main = wgu_in.shape[3] // 2 - 64
    low = lax.broadcasted_iota(jnp.int32, (count * rows, 128), 1) < 64

    def piece(gate, up, given):
        sigma = 1.0 / (1.0 + jnp.exp(-gate))
        act = gate * sigma
        return act * up, given * up * (sigma * (1.0 + gate * (1.0 - sigma))), given * act

    total[...] = jnp.zeros_like(total)

    @pl.loop(0, 2)
    def _(part):
        wgu_ref, wd_ref = wgu_held.at[part], wd_held.at[part]
        for copy in copies(part, 0):
            copy.wait()
        both = nn(h_ref[...], wgu_ref[...])
        for copy in copies(part, 1):
            copy.wait()
        d_inner = nt(c_ref[...], wd_ref[...])
        tile = both[:, main : main + 128]
        inner_m, dg_m, du_m = piece(both[:, :main], both[:, main + 128 :], d_inner[:, :main])
        inner_t, dg_t, du_t = piece(tile, pltpu.roll(tile, 64, 1), d_inner[:, main:])
        inner = jnp.concatenate([inner_m, jnp.where(low, inner_t, 0.0)], axis=1).astype(BF16)
        d_tile = jnp.where(low, dg_t, pltpu.roll(du_t, 64, 1))
        dgu = jnp.concatenate([dg_m, d_tile, du_m], axis=1).astype(BF16)
        dgu_ref[part] = dgu
        inner_ref[part] = inner
        total[0] += nt(dgu, wgu_ref[...])
        total[1] += nn(inner, wd_ref[...])

    for n in range(count):
        two_out[n][...] = total[0, n * rows : (n + 1) * rows, :].astype(BF16)
        fed_out[n][...] = total[1, n * rows : (n + 1) * rows, :].astype(BF16)


def feed(at, hs, cs, weights, down_rows, whole, tokens):
    count = len(hs)
    rows, width = hs[0].shape
    wide = weights[0].shape[3]
    deep = wide // 2 + 64

    def full(dims):
        return pl.BlockSpec(dims, lambda j: (0,) * len(dims))

    outs = pl.pallas_call(
        functools.partial(feed_kernel, count, down_rows),
        grid=(1,),
        in_specs=[full((rows, width))] * (2 * count)
        + [pl.BlockSpec(memory_space=pl.ANY)] * (2 + len(whole)),
        out_specs=[full((rows, width))] * (2 * count)
        + [pl.BlockSpec((count * rows, width), lambda j: (at, 0))] * 2
        + [pl.BlockSpec((2, count * rows, w), lambda j: (0, at, 0)) for w in (wide, deep)],
        out_shape=[shape((rows, width), BF16)] * (2 * count)
        + [shape((tokens, width), BF16)] * 2
        + [shape((2, tokens, w), BF16) for w in (wide, deep)],
        scratch_shapes=[
            pltpu.VMEM((2, width, wide), BF16),
            pltpu.VMEM((2, deep, width), BF16),
            pltpu.VMEM((2, count * rows, width), F32),
            pltpu.SemaphoreType.DMA((4, max(w.shape[0] for w in weights))),
        ],
        input_output_aliases={2 * count + 2 + n: 2 * count + n for n in range(len(whole))},
        compiler_params=pltpu.CompilerParams(
            vmem_limit_bytes=VMEM_LIMIT, dimension_semantics=("arbitrary",)
        ),
        cost_estimate=pl.CostEstimate(
            flops=12 * count * rows * width * wide,
            bytes_accessed=2 * (3 * width * wide + 12 * count * rows * width),
            transcendentals=0,
        ),
        name="feed",
    )(*hs, *cs, *weights, *whole)
    return outs[:count], outs[count : 2 * count], outs[2 * count :]


def inner_swap(value, mask, count):
    return lax.ppermute(value, ("a", "b"), [(r, r ^ mask) for r in range(count)])


def outer_swap(value, mask, count):
    return lax.ppermute(value, "o", [(r, r ^ mask) for r in range(count)])


def swap(value, mask):
    return lax.ppermute(value, ("a", "b", "c"), [(r, r ^ mask) for r in range(GROUP)])


def after(value, *others):
    return lax.optimization_barrier((value, others))[0]


def gather_blocks(value, *others):
    blocks = {0: value}
    for k in (1, 4, 5):
        blocks[k] = swap(value, k)
    if others:
        blocks = after(blocks, *others)
    for k in (0, 1, 4, 5):
        blocks[k ^ 2] = swap(blocks[k], 2)
    return [blocks[k] for k in range(GROUP)]


def near_sums(parts, first=None):
    order = (0, 1, 4, 5)
    far = [swap(parts[k ^ 2], 2) for k in order]
    if first is not None:
        far = list(after(tuple(far), first))
    block = parts[0].shape
    near = call(
        near_kernel,
        [shape(block, F32)] + [shape(block, BF16)] * 3,
        0,
        [*[parts[k] for k in order], *far],
        0,
        "near",
    )
    return [near[0]] + [swap(near[n], order[n]) for n in (1, 2, 3)]


def normalized(values):
    factor = lax.rsqrt(jnp.mean(values * values, axis=-1, keepdims=True) + EPS)
    return values * factor, factor


def norm_back(grad, plain, factor):
    return factor * (grad - plain * jnp.mean(grad * plain, axis=-1, keepdims=True))


def on_device(
    inner_count,
    stream,
    cotangent,
    doc_lengths,
    attention_gain,
    query_weight,
    key_matrix,
    value_matrix,
    query_gain,
    key_gain,
    output_weight,
    feedforward_gain,
    gate_weight,
    up_weight,
    down_weight,
):
    rows, width = stream.shape
    outer, seq = lax.axis_size("o"), GROUP // inner_count
    o = lax.axis_index("o")
    if inner_count == 1:
        i, s = jnp.int32(0), lax.axis_index(("a", "b", "c"))
    else:
        i, s = lax.axis_index(("a", "b")), lax.axis_index("c")
    shards = outer * inner_count
    me = i * seq + s
    tokens = GROUP * rows
    block = rows * seq
    lookback = max(2, -(-DOC_MIN // block))
    halo = lookback * block
    span = 2 * rows
    k_rows = query_weight.shape[0]
    o_rows = output_weight.shape[0]
    ff_rows = down_weight.shape[0] // seq
    ff_local = outer * ff_rows
    main = ff_local - 64
    few = outer <= 4

    def kv_head(i_at, s_at):
        if inner_count == 1:
            return s_at
        return 4 * s_at + 2 * (i_at % 2) + i_at // 2

    shard = o * inner_count + i
    per = query_gain.shape[0]
    meta = jnp.stack([me, o * tokens, shard, s, i, o]).astype(jnp.int32)
    lengths = doc_lengths.astype(jnp.int32)
    gain_one = attention_gain.astype(F32)[:, None]
    gain_two = feedforward_gain.astype(F32)[:, None]
    head_gains = jnp.concatenate([query_gain, key_gain]).astype(F32)

    heads_in = [query_weight, key_matrix, value_matrix, gain_one]
    heads_shape = (inner_count, k_rows + 16, 256)
    chips = ("o", "b")
    if inner_count > 1:
        sent = call(
            functools.partial(send_heads_kernel, kv_head, seq),
            [shape(heads_shape[1:], BF16)] * inner_count,
            2,
            [meta, head_gains, *heads_in],
            0,
            "send_heads",
            [pltpu.VMEM(heads_shape, BF16)],
        )
        (packed,) = call(
            arrange_heads_kernel,
            [shape((outer, *heads_shape), BF16)],
            1,
            [meta, sent[0]] + [inner_swap(sent[m], m, inner_count) for m in range(1, inner_count)],
            0,
            "arrange_heads",
        )
        n_blocks = gather_blocks(normalized(after(stream, packed).astype(F32))[0].astype(BF16))
        w_heads = lax.all_to_all(packed, "o", split_axis=0, concat_axis=0, tiled=True)
        wide_in = after((gate_weight, up_weight), packed)
        sent = call(
            functools.partial(send_wide_kernel, seq, outer),
            [shape((k_rows, 2 * ff_local), BF16)] * inner_count,
            1,
            [meta, *wide_in, gain_two],
            0,
            "send_wide",
            [
                pltpu.VMEM((inner_count, k_rows, 2 * ff_local), BF16),
                pltpu.VMEM((2, k_rows, ff_local), F32),
            ],
        )
        (packed_gu,) = call(
            arrange_wide_kernel,
            [shape((inner_count, k_rows, 2 * ff_local), BF16)],
            1,
            [meta, sent[0]] + [inner_swap(sent[m], m, inner_count) for m in range(1, inner_count)],
            0,
            "arrange_wide",
        )
        half_down = lax.dynamic_slice_in_dim(down_weight, s * ff_rows, ff_rows, 0)
        w_rest = lax.all_gather(jnp.concatenate([half_down, output_weight]), chips, axis=0)
        w_rest = w_rest.reshape(outer, 2, ff_rows + o_rows, width)
        down_rows, w_down = ff_rows, w_rest
        w_out = lax.dynamic_index_in_dim(w_rest, 2 * s + i % 2, 0, keepdims=False)
        w_out = w_out[:, ff_rows:].reshape(128, width)
    else:
        (packed,) = call(
            functools.partial(pack_heads_kernel, kv_head, seq),
            [shape(heads_shape, BF16)],
            2,
            [meta, head_gains, *heads_in],
            0,
            "pack_heads",
        )

        def columns(weight):
            scaled = (weight.astype(F32) * gain_two).astype(BF16)
            split = scaled.reshape(k_rows, outer, seq, ff_rows)
            return lax.dynamic_index_in_dim(split, s, 2, keepdims=False).reshape(k_rows, ff_local)

        gate_c, up_c = columns(gate_weight), columns(up_weight)
        packed_gu = jnp.concatenate(
            [gate_c[:, :main], gate_c[:, main:], up_c[:, main:], up_c[:, :main]], axis=1
        )
        half_down = lax.dynamic_slice_in_dim(down_weight, s * ff_rows, ff_rows, 0)
        w_down = lax.all_gather(half_down, chips, axis=0).reshape(outer, 2, ff_rows, width)
        w_down = w_down.transpose(1, 0, 2, 3).reshape(1, 2, ff_local, width)
        down_rows = ff_local
        n_blocks = gather_blocks(normalized(stream.astype(F32))[0].astype(BF16))
        w_heads = lax.all_gather(packed, "o", axis=0)
        w_out = lax.all_gather(output_weight, "o", axis=0, tiled=True)
        w_out = lax.dynamic_slice_in_dim(w_out, s * 128, 128, 0)
    w_heads = w_heads.reshape(shards, k_rows + 16, 256)
    starts = jnp.cumsum(lengths) - lengths
    places = o * tokens + jnp.arange(tokens, dtype=jnp.int32)
    begin = jnp.max(jnp.where(starts[None, :] <= places[:, None], starts[None, :], -1), axis=1)
    half = HEAD_SIZE // 2
    freq = jnp.power(THETA, -(jnp.arange(half, dtype=F32) * (2.0 / HEAD_SIZE)))
    angle = (places - begin).astype(F32)[:, None] * freq[None, :]
    cosine = jnp.tile(jnp.cos(angle), (1, 4))
    sine = jnp.tile(jnp.sin(angle), (1, 4))

    own_c = after(cotangent, n_blocks[5])
    c_blocks = {0: own_c, 1: swap(own_c, 1), 4: swap(own_c, 4), 5: swap(own_c, 5)}
    hops = -(-halo // tokens)
    blocks_scratch = [
        pltpu.VMEM((GROUP, rows, width), BF16),
        pltpu.SemaphoreType.DMA((GROUP,)),
    ]
    tail_rows = halo - (hops - 1) * tokens
    queries, kv, tail, lin, n_all, w_qkv, head_row = call(
        prepare_kernel,
        [
            shape((2, tokens, 128), BF16),
            shape((tokens, 128), BF16),
            shape((tail_rows, 128), BF16),
            shape((tokens, 256), F32),
            shape((tokens, width), BF16),
            shape((width, 256), BF16),
            shape((8, 256), F32),
        ],
        1,
        [meta, *n_blocks, w_heads, cosine, sine],
        2 * tokens * width * 256,
        "prepare",
        [pltpu.SemaphoreType.DMA((GROUP,))],
        far_in=range(1, GROUP + 1),
    )
    w_gu = lax.all_gather(
        packed_gu.reshape(inner_count * k_rows, 2 * ff_local), chips, axis=0
    ).reshape(outer, 2, inner_count * k_rows, 2 * ff_local)

    keys = [
        lax.ppermute(
            tail if hop == hops else kv, "o", [(at, at + hop) for at in range(max(0, outer - hop))]
        )
        for hop in range(hops, 0, -1)
    ] + [kv]
    steps = tokens // span
    reach = halo + tokens
    pair_flops = 4 * tokens * (span + halo // 2) * 128

    def attention(kernel, ins, outs, scratch, flops, name):
        return pl.pallas_call(
            functools.partial(kernel, halo, span),
            grid=(steps,),
            in_specs=[SM, SM] + [spec for _, spec in ins],
            out_specs=[spec for _, spec in outs],
            out_shape=[dims for dims, _ in outs],
            scratch_shapes=scratch,
            compiler_params=pltpu.CompilerParams(
                vmem_limit_bytes=VMEM_LIMIT, dimension_semantics=("arbitrary",)
            ),
            cost_estimate=pl.CostEstimate(
                flops=flops, bytes_accessed=4 * reach * 256, transcendentals=0
            ),
            name=name,
        )(meta, lengths, *[value for value, _ in ins])

    def still(value):
        return pl.BlockSpec(value.shape, lambda j: (0, 0))

    q_spec = pl.BlockSpec((2, span, 128), lambda j: (0, j, 0))
    row_spec = pl.BlockSpec((span, 128), lambda j: (j, 0))
    log_spec = pl.BlockSpec((8, 2 * span), lambda j: (j, 0))
    key_ins = [(part, still(part)) for part in keys]
    attended, logs = attention(
        attend_kernel,
        [(queries, q_spec), *key_ins],
        [
            (shape((tokens, 128), BF16), row_spec),
            (shape((8 * steps, 2 * span), F32), log_spec),
        ],
        [pltpu.VMEM((reach, 128), BF16)],
        pair_flops,
        "attend",
    )

    attended = after(attended, tuple(c_blocks.values()))
    parts = call(
        project_kernel,
        [shape((rows, width), BF16)] * GROUP,
        1,
        [meta, attended, w_out],
        2 * tokens * 128 * width,
        "project",
        blocks_scratch,
        far_out=range(GROUP),
    )
    near_parts = near_sums(parts)
    middle, plain_two = call(
        middle_kernel,
        [shape((rows, width), F32), shape((rows, width), BF16)],
        0,
        [stream, *near_parts],
        0,
        "middle",
    )

    h_blocks = {0: plain_two}
    for k in (1, 4, 5):
        h_blocks[k] = swap(h_blocks[0], k)
    fed, two, whole = {}, {}, []
    for at, ks in ((2, (0,)), (0, (1, 4)), (3, (5,))):
        fed_k, two_k, whole = feed(
            at,
            [h_blocks[k] for k in ks],
            [c_blocks[k] for k in ks],
            [w_gu, w_down],
            down_rows,
            whole,
            4 * rows,
        )
        for n, k in enumerate(ks):
            fed[k], two[k] = fed_k[n], two_k[n]
    h_all, c_all, dgu_all, inner_all = whole

    def from_chips(parts):
        return [parts[0]] + [swap(parts[k], k) for k in (1, 4, 5)]

    d_mid_f, d_mid = call(
        back_norm_kernel,
        [shape((rows, width), F32), shape((rows, width), BF16)],
        0,
        [middle, cotangent, *from_chips(two)],
        0,
        "back_two",
    )
    if inner_count > 1:
        (grad_gu,) = call(
            wide_grad_kernel,
            [shape((outer, 2, inner_count * k_rows, 2 * ff_local), BF16)],
            0,
            [h_all, dgu_all],
            0,
            "wide_grad",
        )
        grad_gu = after(grad_gu, d_mid).reshape(-1, 2 * ff_local)
        grad_gu = lax.psum_scatter(grad_gu, chips, scatter_dimension=0, tiled=True)
        grad_gu = grad_gu.reshape(inner_count, k_rows, 2 * ff_local)
        (grad_rest,) = call(
            functools.partial(down_grad_kernel, ff_rows),
            [shape((outer, 2, ff_rows + o_rows, width), BF16)],
            0,
            [inner_all, c_all],
            0,
            "down_grad",
        )
        m_blocks = gather_blocks(d_mid, grad_rest)
        d_attended, grad_rest = pl.pallas_call(
            unproject_into_kernel,
            in_specs=[SM] + [FAR] * GROUP + [VM, VM, FAR],
            out_specs=[VM, FAR],
            out_shape=[shape((tokens, 128), BF16), shape(grad_rest.shape, BF16)],
            scratch_shapes=[
                pltpu.VMEM((128, width), BF16),
                pltpu.VMEM((outer, 2, o_rows, width), BF16),
                pltpu.SemaphoreType.DMA(()),
                *blocks_scratch,
            ],
            input_output_aliases={GROUP + 3: 1},
            compiler_params=pltpu.CompilerParams(vmem_limit_bytes=VMEM_LIMIT),
            cost_estimate=pl.CostEstimate(
                flops=4 * tokens * 128 * width, bytes_accessed=8 << 20, transcendentals=0
            ),
            name="unproject",
        )(meta, *m_blocks, w_out, attended, grad_rest)
        grad_rest = grad_rest.reshape(-1, width)
        grad_rest = lax.psum_scatter(grad_rest, chips, scatter_dimension=0, tiled=True)
        grad_down, grad_output = call(
            rest_out_kernel,
            [shape((seq * ff_rows, width), F32), shape((o_rows, width), F32)],
            1,
            [meta, grad_rest, swap(grad_rest, 1)],
            0,
            "rest_out",
        )
    else:
        m_blocks = gather_blocks(d_mid)
        grad_gu = jnp.stack([tn(h_all, dgu_all[n]).astype(BF16) for n in range(2)])
        grad_gu = grad_gu.reshape(2, outer, k_rows, 2 * ff_local).transpose(1, 0, 2, 3)
        grad_gu = lax.psum_scatter(
            grad_gu.reshape(-1, 2 * ff_local), chips, scatter_dimension=0, tiled=True
        ).reshape(inner_count, k_rows, 2 * ff_local)
        d_attended, grad_out = call(
            unproject_kernel,
            [shape((tokens, 128), BF16), shape((128, width), BF16)],
            1,
            [meta, *m_blocks, w_out, attended],
            4 * tokens * 128 * width,
            "unproject",
            blocks_scratch,
            far_in=range(1, GROUP + 1),
        )
        grad_dn = jnp.stack([tn(inner_all[n], c_all)[:ff_local].astype(BF16) for n in range(2)])
        grad_dn = grad_dn.reshape(2, outer, ff_rows, width).transpose(1, 0, 2, 3)
        grad_dn = lax.psum_scatter(
            grad_dn.reshape(-1, width), chips, scatter_dimension=0, tiled=True
        )
        grad_down = lax.all_gather(grad_dn, ("a", "b", "c"), axis=0, tiled=True).astype(F32)
        spot = lax.dynamic_update_slice_in_dim(
            jnp.zeros((shards * o_rows, width), BF16), grad_out, s * 128, 0
        )
        spot = lax.psum_scatter(spot, "o", scatter_dimension=0, tiled=True)
        grad_output = lax.psum(spot, ("a", "b", "c")).astype(F32)

    def to_owners(value):
        value = jnp.repeat(value, seq, axis=0)
        return lax.all_to_all(value, ("a", "b", "c"), split_axis=0, concat_axis=0, tiled=True)

    got = to_owners(grad_gu)
    dq, d_early, d_own = attention(
        attend_back_kernel,
        [
            (queries, q_spec),
            *key_ins,
            (d_attended, row_spec),
            (attended, row_spec),
            (logs, log_spec),
        ],
        [
            (shape((tokens, 128), BF16), row_spec),
            (shape((halo, 128), BF16), pl.BlockSpec((halo, 128), lambda j: (0, 0))),
            (shape((tokens, 128), F32), pl.BlockSpec((tokens, 128), lambda j: (0, 0))),
        ],
        [pltpu.VMEM((reach, 128), BF16), pltpu.VMEM((reach, 128), F32)],
        3 * pair_flops,
        "attend_back",
    )
    late = dict(zip(fed, after(tuple(fed.values()), m_blocks)))
    result = middle
    for part in from_chips(late):
        result = result + part.astype(F32)
    result = result.astype(BF16)
    d_early = after(d_early, result)
    backs = []
    for at, hop in enumerate(range(hops, 0, -1)):
        begin_at = 0 if at == 0 else tail_rows + (at - 1) * tokens
        size = tail_rows if at == 0 else tokens
        backs.append(
            lax.ppermute(
                d_early[begin_at : begin_at + size],
                "o",
                [(p + hop, p) for p in range(max(0, outer - hop))],
            )
        )
    *hidden_parts, dlin, gain_part = call(
        finish_kernel,
        [shape((rows, width), BF16)] * GROUP + [shape((tokens, 256), BF16), shape((8, 256), F32)],
        1,
        [meta, dq, d_own, *backs, lin, cosine, sine, w_qkv, head_row],
        2 * tokens * width * 256,
        "finish",
        [pltpu.VMEM((tokens, 128), F32), pltpu.VMEM((tokens, 256), BF16), *blocks_scratch],
        far_out=range(GROUP),
    )
    pieces = outer if few else 1
    grad_p = call(
        project_grad_kernel,
        [shape((shards // pieces, k_rows + 16, 256), BF16)] * pieces,
        1,
        [meta, n_all, dlin, gain_part],
        2 * tokens * width * 256,
        "project_grad",
        [pltpu.VMEM((width, 256), BF16)],
    )
    near_h = near_sums(hidden_parts, grad_p)
    _, grad_stream = call(
        back_norm_kernel,
        [shape((rows, width), F32), shape((rows, width), BF16)],
        0,
        [stream, d_mid_f, *near_h],
        0,
        "back_one",
    )

    if inner_count > 1:
        grad_gate, grad_up, gain_sum = call(
            functools.partial(unpack_wide_kernel, outer),
            [shape((k_rows, GROUP * ff_local), F32)] * 2 + [shape((k_rows, 128), F32)],
            0,
            [got, gate_weight, up_weight, gain_two],
            0,
            "unpack_wide",
        )
        grad_feedforward_gain = gain_sum[:, 0]
    else:
        gu = got.astype(F32)

        def wide(value):
            split = value.reshape(inner_count, seq, k_rows, outer, ff_rows)
            return split.transpose(2, 3, 0, 1, 4).reshape(k_rows, -1)

        raw_gate = wide(gu[..., :ff_local])
        raw_up = wide(
            jnp.concatenate(
                [gu[..., ff_local + 64 :], gu[..., ff_local : ff_local + 64]], axis=-1
            )
        )
        grad_feedforward_gain = jnp.sum(
            raw_gate * gate_weight.astype(F32) + raw_up * up_weight.astype(F32), axis=1
        )
        grad_gate, grad_up = raw_gate * gain_two, raw_up * gain_two

    if few:
        grad_p = [grad_p[0]] + [outer_swap(grad_p[m], m, outer) for m in range(1, outer)]
        grad_p = after(grad_p, near_h[0], got)
        (total,) = call(
            functools.partial(spread_sum_kernel, seq),
            [shape((GROUP, k_rows + 16, 256), BF16)],
            0,
            grad_p,
            0,
            "spread_sum",
        )
        total = after(total, near_h[1:])
        owned = lax.all_to_all(total, ("a", "b", "c"), split_axis=0, concat_axis=0, tiled=True)
    else:
        owned = to_owners(lax.psum_scatter(grad_p[0], "o", scatter_dimension=0, tiled=True))
    grad_query, grad_key, grad_value, gain_sum, head_sums = call(
        functools.partial(owners_kernel, kv_head, seq, per),
        [
            shape(query_weight.shape, F32),
            shape(key_matrix.shape, F32),
            shape(value_matrix.shape, F32),
            shape((k_rows, 128), F32),
            shape((8, 128), F32),
        ],
        1,
        [meta, owned, query_weight, key_matrix, value_matrix, gain_one],
        0,
        "owners",
    )
    return (
        result,
        grad_stream,
        gain_sum[:, 0],
        grad_query,
        grad_key,
        grad_value,
        head_sums[0, :per],
        head_sums[0, 64 : 64 + per],
        grad_output,
        grad_feedforward_gain,
        grad_gate,
        grad_up,
        grad_down,
    )


def solution(mesh):
    fsdp, seq = mesh.shape["fsdp"], mesh.shape["seq"]
    inner = GROUP // seq
    split = Mesh(mesh.devices.reshape(fsdp // inner, 2, 2, 2), ("o", "a", "b", "c"))
    both = ("o", "a", "b") if inner > 1 else ("o",)
    tokens, matrix, vector = P(("o", "a", "b", "c"), None), P(both, None), P(both)
    placed = (
        tokens,
        tokens,
        P(),
        vector,
        matrix,
        matrix,
        matrix,
        vector,
        vector,
        matrix,
        vector,
        matrix,
        matrix,
        matrix,
    )
    return jax.shard_map(
        functools.partial(on_device, inner),
        mesh=split,
        in_specs=placed,
        out_specs=(
            tokens,
            tokens,
            vector,
            matrix,
            matrix,
            matrix,
            vector,
            vector,
            matrix,
            vector,
            matrix,
            matrix,
            matrix,
        ),
        check_vma=False,
    )
```

profile of v0, /device:TPU:0, one launch (start us, length us, event | category | flops | bytes accessed | tf_op | source)
XLA Modules:
  0.0 359.1 jit_solution(11136604611300710817)
XLA Ops:
  28.7 5.2 %collective-permute-done.22.refs_2_ = bf16[64,1152]{1,0:T(8,128)(2,1)S(1)} collective-permute-done((bf16[64,1152]{1,0:T(8,128)(2,1)}, bf16[64,1152]{1,0:T(8,128)(2,1)S(1)}, u32[]{:S(2)}, u32[]{:S(2)}) %collective-permute-start.22) | collective-permute-done | bytes 147488 | tf_op jit(solution)/shard_map/ppermute | solution.py:657
  38.8 4.9 %all-to-all-start = ((bf16[4,4,80,256]{3,2,1,0:T(8,128)(2,1)}), bf16[4,4,80,256]{3,2,1,0:T(8,128)(2,1)S(1)}, u32[]{:S(2)}, u32[]{:S(2)}) async-start(bf16[4,4,80,256]{3,2,1,0:T(8,128)(2,1)} %arrange_heads.1), calls=%async_computation | async-start | bytes 1310720 | tf_op jit(solution)/shard_map/all_to_all | solution.py:782
  47.8 9.2 %collective-permute-done.7.refs_5_ = bf16[192,1024]{1,0:T(8,128)(2,1)S(1)} collective-permute-done((bf16[192,1024]{1,0:T(8,128)(2,1)S(1)}, bf16[192,1024]{1,0:T(8,128)(2,1)S(1)}, u32[]{:S(2)}, u32[]{:S(2)}) %collective-permute-start.7) | collective-permute-done | bytes 393248 | tf_op jit(solution)/shard_map/ppermute | solution.py:665
  56.9 8.1 %collective-permute-done.6.refs_4_ = bf16[192,1024]{1,0:T(8,128)(2,1)} collective-permute-done((bf16[192,1024]{1,0:T(8,128)(2,1)S(1)}, bf16[192,1024]{1,0:T(8,128)(2,1)}, u32[]{:S(2)}, u32[]{:S(2)}) %collective-permute-start.6) | collective-permute-done | bytes 393248 | tf_op jit(solution)/shard_map/ppermute | solution.py:665
  73.1 9.7 %prepare.1 = (bf16[2,1536,128]{2,1,0:T(8,128)(2,1)}, bf16[1536,128]{1,0:T(8,128)(2,1)}, bf16[1152,128]{1,0:T(8,128)(2,1)}, f32[1536,256]{1,0:T(8,128)}, bf16[153...) custom-call(s32[6]{0:T(128)} %stack.27.meta, bf16[192,1024]{1,0:T(8,128)(2,1)} %copy-done.6, ...), custom_call_target="tpu_custom_call" | custom-call | flops 805306368 | bytes 12099608 | tf_op jit(solution)/shard_map/prepare/pallas_call | solution.py:42
  82.9 3.8 %collective-permute-start.10 = (bf16[1152,128]{1,0:T(8,128)(2,1)}, bf16[1152,128]{1,0:T(8,128)(2,1)S(1)}, u32[]{:S(2)}, u32[]{:S(2)}) collective-permute-start(bf16[1152,128]{1,0:T(8,128)(2,1)} %get-tuple-element.130), channel_id=1, source_target_pairs={{0,8},{8,16},{16,24},{1,9},{9,17},{17,25},{2,10},{10,18},{18,26},{... | collective-permute-start | bytes 884744 | tf_op jit(solution)/shard_map/ppermute | solution.py:878
  86.7 13.2 %collective-permute-done.10.refs_0_ = bf16[1152,128]{1,0:T(8,128)(2,1)S(1)} collective-permute-done((bf16[1152,128]{1,0:T(8,128)(2,1)}, bf16[1152,128]{1,0:T(8,128)(2,1)S(1)}, u32[]{:S(2)}, u32[]{:S(2)}) %collective-permute-start.10) | collective-permute-done | bytes 294944 | tf_op jit(solution)/shard_map/ppermute | solution.py:878
  100.7 8.5 %attend.1 = (bf16[1536,128]{1,0:T(8,128)(2,1)}, f32[32,768]{1,0:T(8,128)}) custom-call(s32[6]{0:T(128)} %stack.27.meta, s32[10]{0:T(128)} %lengths.3, bf16[2,1536,128]{2,1,0:T(8,128)(2,1)} %get-tuple-element.129.q_ref, bf16[1152,128]{1,0:T(8,128)(2,1)} %copy-done.56, bf16[1536,128]{1,0:T(8,128)(2,1)} %get-tuple-element.131.refs_1_), custom_call_target="tpu_custom_call" | custom-call | flops 754974720 | bytes 2752512 | tf_op jit(solution)/shard_map/attend/pallas_call | solution.py:888
  111.6 3.9 %project.1 = (bf16[192,1024]{1,0:T(8,128)(2,1)}, bf16[192,1024]{1,0:T(8,128)(2,1)}, bf16[192,1024]{1,0:T(8,128)(2,1)}, bf16[192,1024]{1,0:T(8,128)(2,1)}, bf16[1...) custom-call(s32[6]{0:T(128)} %stack.27.meta, ...), custom_call_target="tpu_custom_call" | custom-call | flops 402653184 | bytes 3801112 | tf_op jit(solution)/shard_map/project/pallas_call | solution.py:42
  126.7 8.7 %collective-permute-done.18.refs_2_ = bf16[192,1024]{1,0:T(8,128)(2,1)S(1)} collective-permute-done((bf16[192,1024]{1,0:T(8,128)(2,1)}, bf16[192,1024]{1,0:T(8,128)(2,1)S(1)}, u32[]{:S(2)}, u32[]{:S(2)}) %collective-permute-start.18) | collective-permute-done | bytes 393248 | tf_op jit(solution)/shard_map/ppermute | solution.py:665
  135.4 8.4 %collective-permute-done.19.refs_3_ = bf16[192,1024]{1,0:T(8,128)(2,1)S(1)} collective-permute-done((bf16[192,1024]{1,0:T(8,128)(2,1)}, bf16[192,1024]{1,0:T(8,128)(2,1)S(1)}, u32[]{:S(2)}, u32[]{:S(2)}) %collective-permute-start.19) | collective-permute-done | bytes 393248 | tf_op jit(solution)/shard_map/ppermute | solution.py:665
  151.1 9.7 %feed.3 = (bf16[192,1024]{1,0:T(8,128)(2,1)}, bf16[192,1024]{1,0:T(8,128)(2,1)}, bf16[768,1024]{1,0:T(8,128)(2,1)}, bf16[768,1024]{1,0:T(8,128)(2,1)}, bf16[2,76...) custom-call(bf16[192,1024]{1,0:T(8,128)(2,1)} %get-tuple-element.148.refs_0_, bf16[192,1024]{1,0:T(8,128)(2,1)} %refs_1_.2, ...), custom_call_target="tpu_custom_call" | custom-call | flops 2717908992 | bytes 11796480 | tf_op jit(solution)/shard_map/feed/pallas_call | solution.py:625
  161.8 13.7 %feed.4 = (bf16[192,1024]{1,0:T(8,128)(2,1)}, bf16[192,1024]{1,0:T(8,128)(2,1)}, bf16[192,1024]{1,0:T(8,128)(2,1)}, bf16[192,1024]{1,0:T(8,128)(2,1)}, bf16[768,...) custom-call(bf16[192,1024]{1,0:T(8,128)(2,1)} %copy-done.55, ...), custom_call_target="tpu_custom_call", output_to_operand_aliasing={{4}: (6, {}), {5}: (7, {}), {6}: (8, {}), {7}: (9, {})} | custom-call | flops 5435817984 | bytes 16515072 | tf_op jit(solution)/shard_map/feed/pallas_call | solution.py:625
  177.9 9.7 %feed.5 = (bf16[192,1024]{1,0:T(8,128)(2,1)}, bf16[192,1024]{1,0:T(8,128)(2,1)}, bf16[768,1024]{1,0:T(8,128)(2,1)}, bf16[768,1024]{1,0:T(8,128)(2,1)}, bf16[2,76...) custom-call(bf16[192,1024]{1,0:T(8,128)(2,1)} %copy-done.38, ...), custom_call_target="tpu_custom_call", output_to_operand_aliasing={{2}: (4, {}), {3}: (5, {}), {4}: (6, {}), {5}: (7, {})} | custom-call | flops 2717908992 | bytes 11796480 | tf_op jit(solution)/shard_map/feed/pallas_call | solution.py:625
  189.5 10.4 %wide_grad.1 = bf16[4,2,256,1152]{3,2,1,0:T(8,128)(2,1)} custom-call(bf16[768,1024]{1,0:T(8,128)(2,1)} %get-tuple-element.216.h_ref, bf16[2,768,1152]{2,1,0:T(8,128)(2,1)} %get-tuple-element.217.d_ref), custom_call_target="tpu_custom_call" | custom-call | bytes 9830400 | tf_op jit(solution)/shard_map/wide_grad/pallas_call | solution.py:42
  201.0 3.3 back_two.1
  208.7 6.2 %down_grad.1.refs_10_ = bf16[4,2,208,1024]{3,2,1,0:T(8,128)(2,1)} custom-call(bf16[2,768,640]{2,1,0:T(8,128)(2,1)} %get-tuple-element.172.inner_ref, bf16[768,1024]{1,0:T(8,128)(2,1)} %get-tuple-element.173.c_ref), custom_call_target="tpu_custom_call" | custom-call | bytes 6946816 | tf_op jit(solution)/shard_map/down_grad/pallas_call | solution.py:42
  214.9 3.3 collective-permute-done.32.refs_5_
  218.2 4.2 %collective-permute-done.31.refs_4_ = bf16[192,1024]{1,0:T(8,128)(2,1)S(1)} collective-permute-done((bf16[192,1024]{1,0:T(8,128)(2,1)S(1)}, bf16[192,1024]{1,0:T(8,128)(2,1)S(1)}, u32[]{:S(2)}, u32[]{:S(2)}) %collective-permute-start.31) | collective-permute-done | bytes 393248 | tf_op jit(solution)/shard_map/ppermute | solution.py:665
  226.9 7.1 %unproject.1 = (bf16[1536,128]{1,0:T(8,128)(2,1)}, bf16[4,2,208,1024]{3,2,1,0:T(8,128)(2,1)}) custom-call(s32[6]{0:T(128)} %stack.27.meta, bf16[192,1024]{1,0:T(8,128)(2,1)} %get-tuple-element.174.refs_0_, bf16[192,1024]{1,0:T(8,128)(2,1)} %copy-done.12, bf16[192,1024]{1,0:T(8,128)(2,1)} %copy-done.13, ...), custom_call_target="tpu_custom_call", output_to_operand_aliasing={{1}: (11, {})} | custom-call | flops 805306368 | bytes 8388608 | tf_op jit(solution)/shard_map/unproject/pallas_call | solution.py:994
  238.6 12.7 %attend_back.1 = (bf16[1536,128]{1,0:T(8,128)(2,1)}, bf16[1152,128]{1,0:T(8,128)(2,1)}, f32[1536,128]{1,0:T(8,128)}) custom-call(s32[6]{0:T(128)} %stack.27.meta, s32[10]{0:T(128)} %lengths.3, bf16[2,1536,128]{2,1,0:T(8,128)(2,1)} %get-tuple-element.129.q_ref, bf16[1152,128]{1,0:T(8,128)(2,1)} %copy-done.56, bf16[1536,128]{1,0:T(8,128)(2,1)} %get-tuple-element.131.refs_1_, ...), custom_call_target="tpu_custom_call" | custom-call | flops 2264924160 | bytes 2752512 | tf_op jit(solution)/shard_map/attend_back/pallas_call | solution.py:888
  251.3 4.5 %collective-permute-done.38 = bf16[192,1024]{1,0:T(8,128)(2,1)S(1)} collective-permute-done((bf16[192,1024]{1,0:T(8,128)(2,1)S(1)}, bf16[192,1024]{1,0:T(8,128)(2,1)S(1)}, u32[]{:S(2)}, u32[]{:S(2)}) %collective-permute-start.38) | collective-permute-done | bytes 393248 | tf_op jit(solution)/shard_map/ppermute | solution.py:665
  258.1 11.0 %reduce-scatter.3.cloned.1.call-done = bf16[256,1152]{1,0:T(8,128)(2,1)} async-done(((bf16[2048,1152]{1,0:T(8,128)(2,1)}), bf16[256,1152]{1,0:T(8,128)(2,1)}) %reduce-scatter.3.cloned.1.call-update) | async-done | bytes 589840 | tf_op jit(solution)/shard_map/reduce_scatter | solution.py:983
  271.3 3.7 %all-to-all-start.1 = ((bf16[8,64,1152]{2,1,0:T(8,128)(2,1)}), bf16[8,64,1152]{2,1,0:T(8,128)(2,1)S(1)}, u32[]{:S(2)}, u32[]{:S(2)}) async-start(bf16[8,64,1152]{2,1,0:T(8,128)(2,1)} %bitcast.20), calls=%async_computation.2 | async-start | bytes 2359296 | tf_op jit(solution)/shard_map/all_to_all | solution.py:1053
  275.8 10.9 %finish.1 = (bf16[192,1024]{1,0:T(8,128)(2,1)}, bf16[192,1024]{1,0:T(8,128)(2,1)}, bf16[192,1024]{1,0:T(8,128)(2,1)}, bf16[192,1024]{1,0:T(8,128)(2,1)}, bf16[19...) custom-call(s32[6]{0:T(128)} %stack.27.meta, ...), custom_call_target="tpu_custom_call" | custom-call | flops 805306368 | bytes 9093144 | tf_op jit(solution)/shard_map/finish/pallas_call | solution.py:42
  287.8 4.1 %project_grad.1 = (bf16[4,80,256]{2,1,0:T(8,128)(2,1)}, bf16[4,80,256]{2,1,0:T(8,128)(2,1)}, bf16[4,80,256]{2,1,0:T(8,128)(2,1)}, bf16[4,80,256]{2,1,0:T(8,128)(2,1)}) custom-call(s32[6]{0:T(128)} %stack.27.meta, bf16[1536,1024]{1,0:T(8,128)(2,1)} %get-tuple-element.200.n_ref, bf16[1536,256]{1,0:T(8,128)(2,1)} %get-tuple-element.201.d_ref, ...), custom_call_target="tpu_custom_call" | custom-call | flops 805306368 | bytes 4595736 | tf_op jit(solution)/shard_map/project_grad/pallas_call | solution.py:42
  295.8 3.2 near.3
  304.0 15.3 %reduce-scatter.5.cloned.1.call-done.mine_ref = bf16[208,1024]{1,0:T(8,128)(2,1)} async-done(((bf16[1664,1024]{1,0:T(8,128)(2,1)}), bf16[208,1024]{1,0:T(8,128)(2,1)}) %reduce-scatter.5.cloned.1.call-update) | async-done | bytes 426000 | tf_op jit(solution)/shard_map/reduce_scatter | solution.py:1013
  323.7 4.3 %collective-permute-done.50.refs_3_ = bf16[4,80,256]{2,1,0:T(8,128)(2,1)S(1)} collective-permute-done((bf16[4,80,256]{2,1,0:T(8,128)(2,1)S(1)}, bf16[4,80,256]{2,1,0:T(8,128)(2,1)S(1)}, u32[]{:S(2)}, u32[]{:S(2)}) %collective-permute-start.50) | collective-permute-done | bytes 163872 | tf_op jit(solution)/shard_map/ppermute | solution.py:661
  331.5 3.4 all-to-all-start.2
  335.0 3.3 back_one.1
  341.4 4.0 %unpack_wide.1 = (f32[64,4608]{1,0:T(8,128)}, f32[64,4608]{1,0:T(8,128)}, f32[64,128]{1,0:T(8,128)}) custom-call(bf16[8,64,1152]{2,1,0:T(8,128)(2,1)} %copy-done.3, bf16[64,4608]{1,0:T(8,128)(2,1)} %gate_w.1, bf16[64,4608]{1,0:T(8,128)(2,1)} %up_w.1, f32[64,1]{1,0:T(8,128)} %copy.59.scale_ref), custom_call_target="tpu_custom_call" | custom-call | bytes 4751616 | tf_op jit(solution)/shard_map/unpack_wide/pallas_call | solution.py:42
  (270 shorter events, 113.1 us)
Async XLA Ops:
  7.2 102.0 %all-gather.6.cloned.1.call-start = ((), (), s32[]{:S(2)}) async-start(), calls=%async_computation.8 | async-start | bytes 3833856 | tf_op jit(solution)/shard_map/all_gather | solution.py:805
  10.0 141.1 %all-gather.4.cloned.1.call-start = ((), (), s32[]{:S(2)}) async-start(), calls=%async_computation.5 | async-start | bytes 5308416 | tf_op jit(solution)/shard_map/all_gather | solution.py:873
  38.8 33.5 %all-to-all-start = ((bf16[4,4,80,256]{3,2,1,0:T(8,128)(2,1)}), bf16[4,4,80,256]{3,2,1,0:T(8,128)(2,1)S(1)}, u32[]{:S(2)}, u32[]{:S(2)}) async-start(bf16[4,4,80,256]{3,2,1,0:T(8,128)(2,1)} %arrange_heads.1), calls=%async_computation | async-start | bytes 1310720 | tf_op jit(solution)/shard_map/all_to_all | solution.py:782
  43.7 225.4 %reduce-scatter.3.cloned.1.call-start = ((), (), s32[]{:S(2)}) async-start(), calls=%async_computation.6 | async-start | bytes 5308416 | tf_op jit(solution)/shard_map/reduce_scatter | solution.py:983
  45.6 19.4 %collective-permute-start.6 = (bf16[192,1024]{1,0:T(8,128)(2,1)S(1)}, bf16[192,1024]{1,0:T(8,128)(2,1)}, u32[]{:S(2)}, u32[]{:S(2)}) collective-permute-start(bf16[192,1024]{1,0:T(8,128)(2,1)S(1)} %fusion.1.refs_0_), channel_id=1, source_target_pairs={{0,4},{1,5},{2,6},{3,7},{4,0},{5,1},{6,2},{7,3},{8,12},{9,13},{10,... | collective-permute-start | bytes 1179656 | tf_op jit(solution)/shard_map/ppermute | solution.py:665
  47.0 18.1 %collective-permute-start.3 = (bf16[192,1024]{1,0:T(8,128)(2,1)S(1)}, bf16[192,1024]{1,0:T(8,128)(2,1)}, u32[]{:S(2)}, u32[]{:S(2)}) collective-permute-start(bf16[192,1024]{1,0:T(8,128)(2,1)S(1)} %fusion.1.refs_0_), channel_id=1, source_target_pairs={{0,1},{1,0},{2,3},{3,2},{4,5},{5,4},{6,7},{7,6},{8,9},{9,8},{10,11... | collective-permute-start | bytes 1179656 | tf_op jit(solution)/shard_map/ppermute | solution.py:665
  47.7 22.7 %collective-permute-start.4 = (bf16[192,1024]{1,0:T(8,128)(2,1)S(1)}, bf16[192,1024]{1,0:T(8,128)(2,1)}, u32[]{:S(2)}, u32[]{:S(2)}) collective-permute-start(bf16[192,1024]{1,0:T(8,128)(2,1)S(1)} %fusion.1.refs_0_), channel_id=1, source_target_pairs={{0,2},{1,3},{2,0},{3,1},{4,6},{5,7},{6,4},{7,5},{8,10},{9,11},{10,... | collective-permute-start | bytes 1179656 | tf_op jit(solution)/shard_map/ppermute | solution.py:665
  56.9 14.4 %collective-permute-start.9 = (bf16[192,1024]{1,0:T(8,128)(2,1)S(1)}, bf16[192,1024]{1,0:T(8,128)(2,1)}, u32[]{:S(2)}, u32[]{:S(2)}) collective-permute-start(bf16[192,1024]{1,0:T(8,128)(2,1)S(1)} %collective-permute-done.7.refs_5_), channel_id=1, source_target_pairs={{0,2},{1,3},{2,0},{3,1},{4,6},{5,7},{6,4},{7,5},{8,10},{9,11},{10,... | collective-permute-start | bytes 1179656 | tf_op jit(solution)/shard_map/ppermute | solution.py:665
  68.8 40.4 %collective-permute-start.13 = (bf16[192,1024]{1,0:T(8,128)(2,1)S(1)}, bf16[192,1024]{1,0:T(8,128)(2,1)S(1)}, u32[]{:S(2)}, u32[]{:S(2)}) collective-permute-start(bf16[192,1024]{1,0:T(8,128)(2,1)S(1)} %copy-done.31), channel_id=1, source_target_pairs={{0,5},{1,4},{2,7},{3,6},{4,1},{5,0},{6,3},{7,2},{8,13},{9,12},{10,... | collective-permute-start | bytes 1179656 | tf_op jit(solution)/shard_map/ppermute | solution.py:665
  70.4 38.8 %collective-permute-start.12 = (bf16[192,1024]{1,0:T(8,128)(2,1)S(1)}, bf16[192,1024]{1,0:T(8,128)(2,1)S(1)}, u32[]{:S(2)}, u32[]{:S(2)}) collective-permute-start(bf16[192,1024]{1,0:T(8,128)(2,1)S(1)} %copy-done.31), channel_id=1, source_target_pairs={{0,4},{1,5},{2,6},{3,7},{4,0},{5,1},{6,2},{7,3},{8,12},{9,13},{10,... | collective-permute-start | bytes 1179656 | tf_op jit(solution)/shard_map/ppermute | solution.py:665
  71.3 37.9 %collective-permute-start.11 = (bf16[192,1024]{1,0:T(8,128)(2,1)S(1)}, bf16[192,1024]{1,0:T(8,128)(2,1)S(1)}, u32[]{:S(2)}, u32[]{:S(2)}) collective-permute-start(bf16[192,1024]{1,0:T(8,128)(2,1)S(1)} %copy-done.31), channel_id=1, source_target_pairs={{0,1},{1,0},{2,3},{3,2},{4,5},{5,4},{6,7},{7,6},{8,9},{9,8},{10,11... | collective-permute-start | bytes 1179656 | tf_op jit(solution)/shard_map/ppermute | solution.py:665
  82.9 17.0 %collective-permute-start.10 = (bf16[1152,128]{1,0:T(8,128)(2,1)}, bf16[1152,128]{1,0:T(8,128)(2,1)S(1)}, u32[]{:S(2)}, u32[]{:S(2)}) collective-permute-start(bf16[1152,128]{1,0:T(8,128)(2,1)} %get-tuple-element.130), channel_id=1, source_target_pairs={{0,8},{8,16},{16,24},{1,9},{9,17},{17,25},{2,10},{10,18},{18,26},{... | collective-permute-start | bytes 884744 | tf_op jit(solution)/shard_map/ppermute | solution.py:878
  124.3 19.5 %collective-permute-start.19 = (bf16[192,1024]{1,0:T(8,128)(2,1)}, bf16[192,1024]{1,0:T(8,128)(2,1)S(1)}, u32[]{:S(2)}, u32[]{:S(2)}) collective-permute-start(bf16[192,1024]{1,0:T(8,128)(2,1)} %get-tuple-element.145), channel_id=1, source_target_pairs={{0,4},{1,5},{2,6},{3,7},{4,0},{5,1},{6,2},{7,3},{8,12},{9,13},{10,... | collective-permute-start | bytes 1179656 | tf_op jit(solution)/shard_map/ppermute | solution.py:665
  125.5 18.4 %collective-permute-start.20 = (bf16[192,1024]{1,0:T(8,128)(2,1)}, bf16[192,1024]{1,0:T(8,128)(2,1)S(1)}, u32[]{:S(2)}, u32[]{:S(2)}) collective-permute-start(bf16[192,1024]{1,0:T(8,128)(2,1)} %get-tuple-element.146), channel_id=1, source_target_pairs={{0,5},{1,4},{2,7},{3,6},{4,1},{5,0},{6,3},{7,2},{8,13},{9,12},{10,... | collective-permute-start | bytes 1179656 | tf_op jit(solution)/shard_map/ppermute | solution.py:665
  147.6 13.2 %collective-permute-start.25 = (bf16[192,1024]{1,0:T(8,128)(2,1)}, bf16[192,1024]{1,0:T(8,128)(2,1)S(1)}, u32[]{:S(2)}, u32[]{:S(2)}) collective-permute-start(bf16[192,1024]{1,0:T(8,128)(2,1)} %get-tuple-element.148.refs_0_), channel_id=1, source_target_pairs={{0,4},{1,5},{2,6},{3,7},{4,0},{5,1},{6,2},{7,3},{8,12},{9,13},{10,... | collective-permute-start | bytes 1179656 | tf_op jit(solution)/shard_map/ppermute | solution.py:665
  149.2 28.0 %collective-permute-start.26 = (bf16[192,1024]{1,0:T(8,128)(2,1)}, bf16[192,1024]{1,0:T(8,128)(2,1)S(1)}, u32[]{:S(2)}, u32[]{:S(2)}) collective-permute-start(bf16[192,1024]{1,0:T(8,128)(2,1)} %get-tuple-element.148.refs_0_), channel_id=1, source_target_pairs={{0,5},{1,4},{2,7},{3,6},{4,1},{5,0},{6,3},{7,2},{8,13},{9,12},{10,... | collective-permute-start | bytes 1179656 | tf_op jit(solution)/shard_map/ppermute | solution.py:665
  175.5 24.5 %collective-permute-start.27 = (bf16[192,1024]{1,0:T(8,128)(2,1)}, bf16[192,1024]{1,0:T(8,128)(2,1)S(1)}, u32[]{:S(2)}, u32[]{:S(2)}) collective-permute-start(bf16[192,1024]{1,0:T(8,128)(2,1)} %get-tuple-element.168), channel_id=1, source_target_pairs={{0,1},{1,0},{2,3},{3,2},{4,5},{5,4},{6,7},{7,6},{8,9},{9,8},{10,11... | collective-permute-start | bytes 1179656 | tf_op jit(solution)/shard_map/ppermute | solution.py:665
  176.2 23.8 %collective-permute-start.28 = (bf16[192,1024]{1,0:T(8,128)(2,1)}, bf16[192,1024]{1,0:T(8,128)(2,1)S(1)}, u32[]{:S(2)}, u32[]{:S(2)}) collective-permute-start(bf16[192,1024]{1,0:T(8,128)(2,1)} %get-tuple-element.169), channel_id=1, source_target_pairs={{0,4},{1,5},{2,6},{3,7},{4,0},{5,1},{6,2},{7,3},{8,12},{9,13},{10,... | collective-permute-start | bytes 1179656 | tf_op jit(solution)/shard_map/ppermute | solution.py:665
  204.2 115.0 %reduce-scatter.5.cloned.1.call-start = ((), (), s32[]{:S(2)}) async-start(), calls=%async_computation.7 | async-start | bytes 3833856 | tf_op jit(solution)/shard_map/reduce_scatter | solution.py:1013
  206.3 16.1 %collective-permute-start.31 = (bf16[192,1024]{1,0:T(8,128)(2,1)S(1)}, bf16[192,1024]{1,0:T(8,128)(2,1)S(1)}, u32[]{:S(2)}, u32[]{:S(2)}) collective-permute-start(bf16[192,1024]{1,0:T(8,128)(2,1)S(1)} %copy-done.9), channel_id=1, source_target_pairs={{0,4},{1,5},{2,6},{3,7},{4,0},{5,1},{6,2},{7,3},{8,12},{9,13},{10,... | collective-permute-start | bytes 1179656 | tf_op jit(solution)/shard_map/ppermute | solution.py:665
  207.4 15.1 %collective-permute-start.30 = (bf16[192,1024]{1,0:T(8,128)(2,1)S(1)}, bf16[192,1024]{1,0:T(8,128)(2,1)S(1)}, u32[]{:S(2)}, u32[]{:S(2)}) collective-permute-start(bf16[192,1024]{1,0:T(8,128)(2,1)S(1)} %copy-done.9), channel_id=1, source_target_pairs={{0,1},{1,0},{2,3},{3,2},{4,5},{5,4},{6,7},{7,6},{8,9},{9,8},{10,11... | collective-permute-start | bytes 1179656 | tf_op jit(solution)/shard_map/ppermute | solution.py:665
  235.1 16.2 %collective-permute-start.37 = (bf16[192,1024]{1,0:T(8,128)(2,1)S(1)}, bf16[192,1024]{1,0:T(8,128)(2,1)S(1)}, u32[]{:S(2)}, u32[]{:S(2)}) collective-permute-start(bf16[192,1024]{1,0:T(8,128)(2,1)S(1)} %copy-done.52), channel_id=1, source_target_pairs={{0,1},{1,0},{2,3},{3,2},{4,5},{5,4},{6,7},{7,6},{8,9},{9,8},{10,11... | collective-permute-start | bytes 1179656 | tf_op jit(solution)/shard_map/ppermute | solution.py:665
  236.5 19.3 %collective-permute-start.38 = (bf16[192,1024]{1,0:T(8,128)(2,1)S(1)}, bf16[192,1024]{1,0:T(8,128)(2,1)S(1)}, u32[]{:S(2)}, u32[]{:S(2)}) collective-permute-start(bf16[192,1024]{1,0:T(8,128)(2,1)S(1)} %copy-done.51), channel_id=1, source_target_pairs={{0,4},{1,5},{2,6},{3,7},{4,0},{5,1},{6,2},{7,3},{8,12},{9,13},{10,... | collective-permute-start | bytes 1179656 | tf_op jit(solution)/shard_map/ppermute | solution.py:665
  237.2 18.5 %collective-permute-start.39 = (bf16[192,1024]{1,0:T(8,128)(2,1)S(1)}, bf16[192,1024]{1,0:T(8,128)(2,1)S(1)}, u32[]{:S(2)}, u32[]{:S(2)}) collective-permute-start(bf16[192,1024]{1,0:T(8,128)(2,1)S(1)} %copy-done.53), channel_id=1, source_target_pairs={{0,5},{1,4},{2,7},{3,6},{4,1},{5,0},{6,3},{7,2},{8,13},{9,12},{10,... | collective-permute-start | bytes 1179656 | tf_op jit(solution)/shard_map/ppermute | solution.py:665
  256.8 18.2 %collective-permute-start.40 = (bf16[1152,128]{1,0:T(8,128)(2,1)}, bf16[1152,128]{1,0:T(8,128)(2,1)S(1)}, u32[]{:S(2)}, u32[]{:S(2)}) collective-permute-start(bf16[1152,128]{1,0:T(8,128)(2,1)} %get-tuple-element.188), channel_id=1, source_target_pairs={{8,0},{16,8},{24,16},{9,1},{17,9},{25,17},{10,2},{18,10},{26,18},{... | collective-permute-start | bytes 884744 | tf_op jit(solution)/shard_map/ppermute | solution.py:1085
  271.3 56.7 %all-to-all-start.1 = ((bf16[8,64,1152]{2,1,0:T(8,128)(2,1)}), bf16[8,64,1152]{2,1,0:T(8,128)(2,1)S(1)}, u32[]{:S(2)}, u32[]{:S(2)}) async-start(bf16[8,64,1152]{2,1,0:T(8,128)(2,1)} %bitcast.20), calls=%async_computation.2 | async-start | bytes 2359296 | tf_op jit(solution)/shard_map/all_to_all | solution.py:1053
  299.0 31.7 %collective-permute-start.45 = (bf16[192,1024]{1,0:T(8,128)(2,1)}, bf16[192,1024]{1,0:T(8,128)(2,1)S(1)}, u32[]{:S(2)}, u32[]{:S(2)}) collective-permute-start(bf16[192,1024]{1,0:T(8,128)(2,1)} %get-tuple-element.212), channel_id=1, source_target_pairs={{0,1},{1,0},{2,3},{3,2},{4,5},{5,4},{6,7},{7,6},{8,9},{9,8},{10,11... | collective-permute-start | bytes 1179656 | tf_op jit(solution)/shard_map/ppermute | solution.py:665
  299.5 31.2 %collective-permute-start.46 = (bf16[192,1024]{1,0:T(8,128)(2,1)}, bf16[192,1024]{1,0:T(8,128)(2,1)S(1)}, u32[]{:S(2)}, u32[]{:S(2)}) collective-permute-start(bf16[192,1024]{1,0:T(8,128)(2,1)} %get-tuple-element.213), channel_id=1, source_target_pairs={{0,4},{1,5},{2,6},{3,7},{4,0},{5,1},{6,2},{7,3},{8,12},{9,13},{10,... | collective-permute-start | bytes 1179656 | tf_op jit(solution)/shard_map/ppermute | solution.py:665
  301.1 29.6 %collective-permute-start.47 = (bf16[192,1024]{1,0:T(8,128)(2,1)}, bf16[192,1024]{1,0:T(8,128)(2,1)S(1)}, u32[]{:S(2)}, u32[]{:S(2)}) collective-permute-start(bf16[192,1024]{1,0:T(8,128)(2,1)} %get-tuple-element.214), channel_id=1, source_target_pairs={{0,5},{1,4},{2,7},{3,6},{4,1},{5,0},{6,3},{7,2},{8,13},{9,12},{10,... | collective-permute-start | bytes 1179656 | tf_op jit(solution)/shard_map/ppermute | solution.py:665
  302.5 18.3 %collective-permute-start.49 = (bf16[4,80,256]{2,1,0:T(8,128)(2,1)S(1)}, bf16[4,80,256]{2,1,0:T(8,128)(2,1)S(1)}, u32[]{:S(2)}, u32[]{:S(2)}) collective-permute-start(bf16[4,80,256]{2,1,0:T(8,128)(2,1)S(1)} %copy-done.58), channel_id=1, source_target_pairs={{0,16},{8,24},{16,0},{24,8},{1,17},{9,25},{17,1},{25,9},{2,18},{10... | collective-permute-start | bytes 491528 | tf_op jit(solution)/shard_map/ppermute | solution.py:661
  319.3 19.1 %collective-permute-start.51 = (bf16[208,1024]{1,0:T(8,128)(2,1)}, bf16[208,1024]{1,0:T(8,128)(2,1)S(1)}, u32[]{:S(2)}, u32[]{:S(2)}) collective-permute-start(bf16[208,1024]{1,0:T(8,128)(2,1)} %reduce-scatter.5.cloned.1.call-done.mine_ref), channel_id=1, source_target_pairs={{0,1},{1,0},{2,3},{3,2},{4,5},{5,4},{6,7},{7,6},{8,9},{9,8},{10,11... | collective-permute-start | bytes 1277960 | tf_op jit(solution)/shard_map/ppermute | solution.py:665
  331.5 15.3 %all-to-all-start.2 = ((bf16[8,80,256]{2,1,0:T(8,128)(2,1)}), bf16[8,80,256]{2,1,0:T(8,128)(2,1)S(1)}, u32[]{:S(2)}, u32[]{:S(2)}) async-start(bf16[8,80,256]{2,1,0:T(8,128)(2,1)} %spread_sum.1), calls=%async_computation.3 | async-start | bytes 655360 | tf_op jit(solution)/shard_map/all_to_all | solution.py:1161
  (90 other events, 531.5 us)
Sparse Core Ops, SparseCore 0:
  10.1 48.5 all-gather.5
  60.3 51.7 all-gather.3
  204.4 64.7 reduce-scatter.2
  271.3 47.9 reduce-scatter.4
where the time goes:
time: 360 us; the launch traced here: 359 us
  Pallas kernels  142 us (39%)
  waiting for transfers between devices  106 us (29%)
  starting transfers between devices  62.6 us (17%)
  local copies, waits for them, and re-layouts  28.7 us (8%)
  between operations  14.4 us (4%)
  other arithmetic  5.36 us (1%)
    pallas_call x19, Pallas kernels, call(): pl.pallas_call(kernel, out_shape=outs, in_specs=[SM if n < n_smem else FA...  80.3 us
    ppermute x41, waiting for transfers between devices, swap(): lax.ppermute(value, ('a', 'b', 'c'), [(r, r ^ mask) for r in range(GROUP)])  51.7 us
    ppermute x41, starting transfers between devices, swap(): lax.ppermute(value, ('a', 'b', 'c'), [(r, r ^ mask) for r in range(GROUP)])  33.5 us
    pallas_call x3, Pallas kernels, feed(): pl.pallas_call(functools.partial(feed_kernel, count, down_rows), grid=(1,...  33 us
    pallas_call x2, Pallas kernels, attention(): pl.pallas_call(functools.partial(kernel, halo, span), grid=(steps,), in_s...  21.2 us
    unnamed x126, local copies, waits for them, and re-layouts  15.7 us
    reduce_scatter x1, waiting for transfers between devices, on_device(): lax.psum_scatter(grad_rest, chips, scatter_dimension=0, tiled=True)  15.3 us
    ppermute x1, waiting for transfers between devices, on_device(): lax.ppermute(tail if hop == hops else kv, 'o', [(at, at + hop) for at in...  13.2 us
  transfers between devices with their start and end apart: 59, of which 25 were waited for; matrix products, arithmetic and copies ran while one was open for 4% of the time, Pallas kernels for 38%

commit v1 on v0

--- a/solution.py
+++ b/solution.py
@@ -780,27 +780,6 @@
         )
         n_blocks = gather_blocks(normalized(after(stream, packed).astype(F32))[0].astype(BF16))
         w_heads = lax.all_to_all(packed, "o", split_axis=0, concat_axis=0, tiled=True)
-        wide_in = after((gate_weight, up_weight), packed)
-        sent = call(
-            functools.partial(send_wide_kernel, seq, outer),
-            [shape((k_rows, 2 * ff_local), BF16)] * inner_count,
-            1,
-            [meta, *wide_in, gain_two],
-            0,
-            "send_wide",
-            [
-                pltpu.VMEM((inner_count, k_rows, 2 * ff_local), BF16),
-                pltpu.VMEM((2, k_rows, ff_local), F32),
-            ],
-        )
-        (packed_gu,) = call(
-            arrange_wide_kernel,
-            [shape((inner_count, k_rows, 2 * ff_local), BF16)],
-            1,
-            [meta, sent[0]] + [inner_swap(sent[m], m, inner_count) for m in range(1, inner_count)],
-            0,
-            "arrange_wide",
-        )
         half_down = lax.dynamic_slice_in_dim(down_weight, s * ff_rows, ff_rows, 0)
         w_rest = lax.all_gather(jnp.concatenate([half_down, output_weight]), chips, axis=0)
         w_rest = w_rest.reshape(outer, 2, ff_rows + o_rows, width)
@@ -870,16 +849,75 @@
         [pltpu.SemaphoreType.DMA((GROUP,))],
         far_in=range(1, GROUP + 1),
     )
+    starts = jnp.cumsum(lengths) - lengths
+    places = o * tokens + jnp.arange(tokens, dtype=jnp.int32)
+    begin = jnp.max(jnp.where(starts[None, :] <= places[:, None], starts[None, :], -1), axis=1)
+    half = HEAD_SIZE // 2
+    freq = jnp.power(THETA, -(jnp.arange(half, dtype=F32) * (2.0 / HEAD_SIZE)))
+    angle = (places - begin).astype(F32)[:, None] * freq[None, :]
+    cosine = jnp.tile(jnp.cos(angle), (1, 4))
+    sine = jnp.tile(jnp.sin(angle), (1, 4))
+
+    own_c = after(cotangent, n_blocks[5])
+    c_blocks = {0: own_c, 1: swap(own_c, 1), 4: swap(own_c, 4), 5: swap(own_c, 5)}
+    hops = -(-halo // tokens)
+    blocks_scratch = [
+        pltpu.VMEM((GROUP, rows, width), BF16),
+        pltpu.SemaphoreType.DMA((GROUP,)),
+    ]
+    tail_rows = halo - (hops - 1) * tokens
+    queries, kv, tail, lin, n_all, w_qkv, head_row = call(
+        prepare_kernel,
+        [
+            shape((2, tokens, 128), BF16),
+            shape((tokens, 128), BF16),
+            shape((tail_rows, 128), BF16),
+            shape((tokens, 256), F32),
+            shape((tokens, width), BF16),
+            shape((width, 256), BF16),
+            shape((8, 256), F32),
+        ],
+        1,
+        [meta, *n_blocks, w_heads, cosine, sine],
+        2 * tokens * width * 256,
+        "prepare",
+        [pltpu.SemaphoreType.DMA((GROUP,))],
+        far_in=range(1, GROUP + 1),
+    )
+    tail = after(tail, tuple(c_blocks.values()))
+    keys = [
+        lax.ppermute(
+            tail if hop == hops else kv, "o", [(at, at + hop) for at in range(max(0, outer - hop))]
+        )
+        for hop in range(hops, 0, -1)
+    ] + [kv]
+    if inner_count > 1:
+        wide_in = after((gate_weight, up_weight), packed)
+        sent = call(
+            functools.partial(send_wide_kernel, seq, outer),
+            [shape((k_rows, 2 * ff_local), BF16)] * inner_count,
+            1,
+            [meta, *wide_in, gain_two],
+            0,
+            "send_wide",
+            [
+                pltpu.VMEM((inner_count, k_rows, 2 * ff_local), BF16),
+                pltpu.VMEM((2, k_rows, ff_local), F32),
+            ],
+        )
+        sent = [sent[0]] + [inner_swap(sent[m], m, inner_count) for m in range(1, inner_count)]
+    if inner_count > 1:
+        (packed_gu,) = call(
+            arrange_wide_kernel,
+            [shape((inner_count, k_rows, 2 * ff_local), BF16)],
+            1,
+            [meta, *after(sent, keys[0])],
+            0,
+            "arrange_wide",
+        )
     w_gu = lax.all_gather(
         packed_gu.reshape(inner_count * k_rows, 2 * ff_local), chips, axis=0
     ).reshape(outer, 2, inner_count * k_rows, 2 * ff_local)
-
-    keys = [
-        lax.ppermute(
-            tail if hop == hops else kv, "o", [(at, at + hop) for at in range(max(0, outer - hop))]
-        )
-        for hop in range(hops, 0, -1)
-    ] + [kv]
     steps = tokens // span
     reach = halo + tokens
     pair_flops = 4 * tokens * (span + halo // 2) * 128
@@ -920,7 +958,6 @@
         "attend",
     )
 
-    attended = after(attended, tuple(c_blocks.values()))
     parts = call(
         project_kernel,
         [shape((rows, width), BF16)] * GROUP,
@@ -1071,12 +1108,11 @@
         3 * pair_flops,
         "attend_back",
     )
-    late = dict(zip(fed, after(tuple(fed.values()), m_blocks)))
+    late = dict(zip(fed, after(tuple(fed.values()), dq)))
     result = middle
     for part in from_chips(late):
         result = result + part.astype(F32)
     result = result.astype(BF16)
-    d_early = after(d_early, result)
     backs = []
     for at, hop in enumerate(range(hops, 0, -1)):
         begin_at = 0 if at == 0 else tail_rows + (at - 1) * tokens
@@ -1108,7 +1144,7 @@
         "project_grad",
         [pltpu.VMEM((width, 256), BF16)],
     )
-    near_h = near_sums(hidden_parts, grad_p)
+    near_h = near_sums(hidden_parts, (grad_p, result))
     _, grad_stream = call(
         back_norm_kernel,
         [shape((rows, width), F32), shape((rows, width), BF16)],

time: 360 us -> 344 us (0.956)
  waiting for transfers between devices: 106 us -> 90.5 us
  starting transfers between devices: 62.6 us -> 56.9 us
  Pallas kernels: 142 us -> 146 us
    ppermute x1, waiting for transfers between devices: 13.2 us -> 0.01 us  [on_device(): lax.ppermute(tail if hop == hops else kv, 'o', [(at, at + hop) for at in...]
    all_to_all x1, waiting for transfers between devices: 0.01 us -> 12.9 us  [on_device(): lax.all_to_all(packed, 'o', split_axis=0, concat_axis=0, tiled=True)]
    ppermute x41, waiting for transfers between devices: 51.7 us -> 42.2 us  [swap(): lax.ppermute(value, ('a', 'b', 'c'), [(r, r ^ mask) for r in range(GROUP)])]
    reduce_scatter x1, waiting for transfers between devices: 11 us -> 3.73 us  [on_device(): grad_gu = lax.psum_scatter(grad_gu, chips, scatter_dimension=0, tiled=True)]
    ppermute x3, starting transfers between devices: 6.89 us -> 2.48 us  [outer_swap(): return lax.ppermute(value, 'o', [(r, r ^ mask) for r in range(count)])]
  transfers between devices with their start and end apart: 59 -> 59, of which waited for: 25 -> 25; matrix products, arithmetic and copies ran while one was open for 4% -> 4% of each run, Pallas kernels for 38% -> 41%
where the time goes in v1:
time: 344 us; the launch traced here: 342 us
  Pallas kernels  146 us (42%)
  waiting for transfers between devices  90.5 us (26%)
  starting transfers between devices  56.9 us (17%)
  local copies, waits for them, and re-layouts  27.9 us (8%)
  between operations  14.5 us (4%)
  other arithmetic  6.77 us (2%)
    pallas_call x19, Pallas kernels, call(): pl.pallas_call(kernel, out_shape=outs, in_specs=[SM if n < n_smem else FA...  80.7 us
    ppermute x41, waiting for transfers between devices, swap(): lax.ppermute(value, ('a', 'b', 'c'), [(r, r ^ mask) for r in range(GROUP)])  42.2 us
    ppermute x41, starting transfers between devices, swap(): lax.ppermute(value, ('a', 'b', 'c'), [(r, r ^ mask) for r in range(GROUP)])  34.6 us
    pallas_call x3, Pallas kernels, feed(): pl.pallas_call(functools.partial(feed_kernel, count, down_rows), grid=(1,...  33 us
    pallas_call x2, Pallas kernels, attention(): pl.pallas_call(functools.partial(kernel, halo, span), grid=(steps,), in_s...  24.8 us
    unnamed x126, local copies, waits for them, and re-layouts  15.2 us
    reduce_scatter x1, waiting for transfers between devices, on_device(): lax.psum_scatter(grad_rest, chips, scatter_dimension=0, tiled=True)  13.2 us
    all_to_all x1, waiting for transfers between devices, on_device(): lax.all_to_all(packed, 'o', split_axis=0, concat_axis=0, tiled=True)  12.9 us
  transfers between devices with their start and end apart: 59, of which 25 were waited for; matrix products, arithmetic and copies ran while one was open for 4% of the time, Pallas kernels for 41%

profile of v1, /device:TPU:0, one launch (start us, length us, event | category | flops | bytes accessed | tf_op | source)
XLA Modules:
  0.0 342.2 jit_solution(1044301177520430760)
XLA Ops:
  26.0 4.9 %all-to-all-start = ((bf16[4,4,80,256]{3,2,1,0:T(8,128)(2,1)}), bf16[4,4,80,256]{3,2,1,0:T(8,128)(2,1)S(1)}, u32[]{:S(2)}, u32[]{:S(2)}) async-start(bf16[4,4,80,256]{3,2,1,0:T(8,128)(2,1)} %arrange_heads.1), calls=%async_computation | async-start | bytes 1310720 | tf_op jit(solution)/shard_map/all_to_all | solution.py:782
  32.7 4.0 %collective-permute-done.7.refs_5_ = bf16[192,1024]{1,0:T(8,128)(2,1)S(1)} collective-permute-done((bf16[192,1024]{1,0:T(8,128)(2,1)S(1)}, bf16[192,1024]{1,0:T(8,128)(2,1)S(1)}, u32[]{:S(2)}, u32[]{:S(2)}) %collective-permute-start.7) | collective-permute-done | bytes 393248 | tf_op jit(solution)/shard_map/ppermute | solution.py:665
  38.9 6.3 %collective-permute-done.6.refs_4_ = bf16[192,1024]{1,0:T(8,128)(2,1)} collective-permute-done((bf16[192,1024]{1,0:T(8,128)(2,1)S(1)}, bf16[192,1024]{1,0:T(8,128)(2,1)}, u32[]{:S(2)}, u32[]{:S(2)}) %collective-permute-start.6) | collective-permute-done | bytes 393248 | tf_op jit(solution)/shard_map/ppermute | solution.py:665
  51.4 12.9 %all-to-all-done = bf16[4,4,80,256]{3,2,1,0:T(8,128)(2,1)S(1)} async-done(((bf16[4,4,80,256]{3,2,1,0:T(8,128)(2,1)}), bf16[4,4,80,256]{3,2,1,0:T(8,128)(2,1)S(1)}, u32[]{:S(2)}, u32[]{:S(2)}) %all-to-all-start) | async-done | bytes 655392 | tf_op jit(solution)/shard_map/all_to_all | solution.py:782
  65.2 9.8 %prepare.1 = (bf16[2,1536,128]{2,1,0:T(8,128)(2,1)}, bf16[1536,128]{1,0:T(8,128)(2,1)}, bf16[1152,128]{1,0:T(8,128)(2,1)}, f32[1536,256]{1,0:T(8,128)}, bf16[153...) custom-call(s32[6]{0:T(128)} %stack.27.meta, bf16[192,1024]{1,0:T(8,128)(2,1)} %copy-done.6, ...), custom_call_target="tpu_custom_call" | custom-call | flops 805306368 | bytes 12099608 | tf_op jit(solution)/shard_map/prepare/pallas_call | solution.py:42
  77.1 3.1 send_wide.1
  82.0 5.0 %collective-permute-done.22.refs_2_ = bf16[64,1152]{1,0:T(8,128)(2,1)S(1)} collective-permute-done((bf16[64,1152]{1,0:T(8,128)(2,1)}, bf16[64,1152]{1,0:T(8,128)(2,1)S(1)}, u32[]{:S(2)}, u32[]{:S(2)}) %collective-permute-start.22) | collective-permute-done | bytes 147488 | tf_op jit(solution)/shard_map/ppermute | solution.py:657
  92.4 10.0 %attend.1 = (bf16[1536,128]{1,0:T(8,128)(2,1)}, f32[32,768]{1,0:T(8,128)}) custom-call(s32[6]{0:T(128)} %stack.27.meta, s32[10]{0:T(128)} %lengths.3, bf16[2,1536,128]{2,1,0:T(8,128)(2,1)} %get-tuple-element.132.q_ref, bf16[1152,128]{1,0:T(8,128)(2,1)} %copy-done.56, bf16[1536,128]{1,0:T(8,128)(2,1)} %get-tuple-element.136.refs_1_), custom_call_target="tpu_custom_call" | custom-call | flops 754974720 | bytes 2752512 | tf_op jit(solution)/shard_map/attend/pallas_call | solution.py:926
  104.3 3.9 %project.1 = (bf16[192,1024]{1,0:T(8,128)(2,1)}, bf16[192,1024]{1,0:T(8,128)(2,1)}, bf16[192,1024]{1,0:T(8,128)(2,1)}, bf16[192,1024]{1,0:T(8,128)(2,1)}, bf16[1...) custom-call(s32[6]{0:T(128)} %stack.27.meta, ...), custom_call_target="tpu_custom_call" | custom-call | flops 402653184 | bytes 3801112 | tf_op jit(solution)/shard_map/project/pallas_call | solution.py:42
  112.9 3.2 near.2
  119.7 8.7 %collective-permute-done.18.refs_2_ = bf16[192,1024]{1,0:T(8,128)(2,1)S(1)} collective-permute-done((bf16[192,1024]{1,0:T(8,128)(2,1)}, bf16[192,1024]{1,0:T(8,128)(2,1)S(1)}, u32[]{:S(2)}, u32[]{:S(2)}) %collective-permute-start.18) | collective-permute-done | bytes 393248 | tf_op jit(solution)/shard_map/ppermute | solution.py:665
  128.3 7.4 %collective-permute-done.19.refs_3_ = bf16[192,1024]{1,0:T(8,128)(2,1)S(1)} collective-permute-done((bf16[192,1024]{1,0:T(8,128)(2,1)}, bf16[192,1024]{1,0:T(8,128)(2,1)S(1)}, u32[]{:S(2)}, u32[]{:S(2)}) %collective-permute-start.19) | collective-permute-done | bytes 393248 | tf_op jit(solution)/shard_map/ppermute | solution.py:665
  144.0 9.7 %feed.3 = (bf16[192,1024]{1,0:T(8,128)(2,1)}, bf16[192,1024]{1,0:T(8,128)(2,1)}, bf16[768,1024]{1,0:T(8,128)(2,1)}, bf16[768,1024]{1,0:T(8,128)(2,1)}, bf16[2,76...) custom-call(bf16[192,1024]{1,0:T(8,128)(2,1)} %get-tuple-element.151.refs_0_, bf16[192,1024]{1,0:T(8,128)(2,1)} %refs_1_.2, ...), custom_call_target="tpu_custom_call" | custom-call | flops 2717908992 | bytes 11796480 | tf_op jit(solution)/shard_map/feed/pallas_call | solution.py:625
  154.9 13.7 %feed.4 = (bf16[192,1024]{1,0:T(8,128)(2,1)}, bf16[192,1024]{1,0:T(8,128)(2,1)}, bf16[192,1024]{1,0:T(8,128)(2,1)}, bf16[192,1024]{1,0:T(8,128)(2,1)}, bf16[768,...) custom-call(bf16[192,1024]{1,0:T(8,128)(2,1)} %copy-done.55, ...), custom_call_target="tpu_custom_call", output_to_operand_aliasing={{4}: (6, {}), {5}: (7, {}), {6}: (8, {}), {7}: (9, {})} | custom-call | flops 5435817984 | bytes 16515072 | tf_op jit(solution)/shard_map/feed/pallas_call | solution.py:625
  171.5 9.7 %feed.5 = (bf16[192,1024]{1,0:T(8,128)(2,1)}, bf16[192,1024]{1,0:T(8,128)(2,1)}, bf16[768,1024]{1,0:T(8,128)(2,1)}, bf16[768,1024]{1,0:T(8,128)(2,1)}, bf16[2,76...) custom-call(bf16[192,1024]{1,0:T(8,128)(2,1)} %copy-done.41, ...), custom_call_target="tpu_custom_call", output_to_operand_aliasing={{2}: (4, {}), {3}: (5, {}), {4}: (6, {}), {5}: (7, {})} | custom-call | flops 2717908992 | bytes 11796480 | tf_op jit(solution)/shard_map/feed/pallas_call | solution.py:625
  182.6 10.4 %wide_grad.1 = bf16[4,2,256,1152]{3,2,1,0:T(8,128)(2,1)} custom-call(bf16[768,1024]{1,0:T(8,128)(2,1)} %get-tuple-element.222.h_ref, bf16[2,768,1152]{2,1,0:T(8,128)(2,1)} %get-tuple-element.223.d_ref), custom_call_target="tpu_custom_call" | custom-call | bytes 9830400 | tf_op jit(solution)/shard_map/wide_grad/pallas_call | solution.py:42
  194.1 3.2 back_two.1
  201.8 6.6 %down_grad.1.refs_10_ = bf16[4,2,208,1024]{3,2,1,0:T(8,128)(2,1)} custom-call(bf16[2,768,640]{2,1,0:T(8,128)(2,1)} %get-tuple-element.179.inner_ref, bf16[768,1024]{1,0:T(8,128)(2,1)} %get-tuple-element.180.c_ref), custom_call_target="tpu_custom_call" | custom-call | bytes 6946816 | tf_op jit(solution)/shard_map/down_grad/pallas_call | solution.py:42
  208.4 2.9 collective-permute-done.32.refs_5_
  211.3 5.9 %collective-permute-done.31.refs_4_ = bf16[192,1024]{1,0:T(8,128)(2,1)S(1)} collective-permute-done((bf16[192,1024]{1,0:T(8,128)(2,1)S(1)}, bf16[192,1024]{1,0:T(8,128)(2,1)S(1)}, u32[]{:S(2)}, u32[]{:S(2)}) %collective-permute-start.31) | collective-permute-done | bytes 393248 | tf_op jit(solution)/shard_map/ppermute | solution.py:665
  221.6 7.1 %unproject.1 = (bf16[1536,128]{1,0:T(8,128)(2,1)}, bf16[4,2,208,1024]{3,2,1,0:T(8,128)(2,1)}) custom-call(s32[6]{0:T(128)} %stack.27.meta, bf16[192,1024]{1,0:T(8,128)(2,1)} %get-tuple-element.181.refs_0_, bf16[192,1024]{1,0:T(8,128)(2,1)} %copy-done.12, bf16[192,1024]{1,0:T(8,128)(2,1)} %copy-done.13, ...), custom_call_target="tpu_custom_call", output_to_operand_aliasing={{1}: (11, {})} | custom-call | flops 805306368 | bytes 8388608 | tf_op jit(solution)/shard_map/unproject/pallas_call | solution.py:1031
  228.8 14.9 %attend_back.1 = (bf16[1536,128]{1,0:T(8,128)(2,1)}, bf16[1152,128]{1,0:T(8,128)(2,1)}, f32[1536,128]{1,0:T(8,128)}) custom-call(s32[6]{0:T(128)} %stack.27.meta, s32[10]{0:T(128)} %lengths.3, bf16[2,1536,128]{2,1,0:T(8,128)(2,1)} %get-tuple-element.132.q_ref, bf16[1152,128]{1,0:T(8,128)(2,1)} %copy-done.56, bf16[1536,128]{1,0:T(8,128)(2,1)} %get-tuple-element.136.refs_1_, ...), custom_call_target="tpu_custom_call" | custom-call | flops 2264924160 | bytes 2752512 | tf_op jit(solution)/shard_map/attend_back/pallas_call | solution.py:926
  248.5 3.7 %reduce-scatter.3.cloned.1.call-done = bf16[256,1152]{1,0:T(8,128)(2,1)} async-done(((bf16[2048,1152]{1,0:T(8,128)(2,1)}), bf16[256,1152]{1,0:T(8,128)(2,1)}) %reduce-scatter.3.cloned.1.call-update) | async-done | bytes 589840 | tf_op jit(solution)/shard_map/reduce_scatter | solution.py:1020
  254.5 3.7 %all-to-all-start.1 = ((bf16[8,64,1152]{2,1,0:T(8,128)(2,1)}), bf16[8,64,1152]{2,1,0:T(8,128)(2,1)S(1)}, u32[]{:S(2)}, u32[]{:S(2)}) async-start(bf16[8,64,1152]{2,1,0:T(8,128)(2,1)} %bitcast.20), calls=%async_computation.2 | async-start | bytes 2359296 | tf_op jit(solution)/shard_map/all_to_all | solution.py:1090
  258.9 10.8 %finish.1 = (bf16[192,1024]{1,0:T(8,128)(2,1)}, bf16[192,1024]{1,0:T(8,128)(2,1)}, bf16[192,1024]{1,0:T(8,128)(2,1)}, bf16[192,1024]{1,0:T(8,128)(2,1)}, bf16[19...) custom-call(s32[6]{0:T(128)} %stack.27.meta, ...), custom_call_target="tpu_custom_call" | custom-call | flops 805306368 | bytes 9093144 | tf_op jit(solution)/shard_map/finish/pallas_call | solution.py:42
  272.4 4.2 %project_grad.1 = (bf16[4,80,256]{2,1,0:T(8,128)(2,1)}, bf16[4,80,256]{2,1,0:T(8,128)(2,1)}, bf16[4,80,256]{2,1,0:T(8,128)(2,1)}, bf16[4,80,256]{2,1,0:T(8,128)(2,1)}) custom-call(s32[6]{0:T(128)} %stack.27.meta, bf16[1536,1024]{1,0:T(8,128)(2,1)} %get-tuple-element.206.n_ref, bf16[1536,256]{1,0:T(8,128)(2,1)} %get-tuple-element.207.d_ref, ...), custom_call_target="tpu_custom_call" | custom-call | flops 805306368 | bytes 4595736 | tf_op jit(solution)/shard_map/project_grad/pallas_call | solution.py:42
  280.6 3.2 near.3
  289.2 13.2 %reduce-scatter.5.cloned.1.call-done.mine_ref = bf16[208,1024]{1,0:T(8,128)(2,1)} async-done(((bf16[1664,1024]{1,0:T(8,128)(2,1)}), bf16[208,1024]{1,0:T(8,128)(2,1)}) %reduce-scatter.5.cloned.1.call-update) | async-done | bytes 426000 | tf_op jit(solution)/shard_map/reduce_scatter | solution.py:1050
  304.0 7.2 %collective-permute-done.50.refs_3_ = bf16[4,80,256]{2,1,0:T(8,128)(2,1)S(1)} collective-permute-done((bf16[4,80,256]{2,1,0:T(8,128)(2,1)S(1)}, bf16[4,80,256]{2,1,0:T(8,128)(2,1)S(1)}, u32[]{:S(2)}, u32[]{:S(2)}) %collective-permute-start.50) | collective-permute-done | bytes 163872 | tf_op jit(solution)/shard_map/ppermute | solution.py:661
  314.6 3.4 %all-to-all-start.2 = ((bf16[8,80,256]{2,1,0:T(8,128)(2,1)}), bf16[8,80,256]{2,1,0:T(8,128)(2,1)S(1)}, u32[]{:S(2)}, u32[]{:S(2)}) async-start(bf16[8,80,256]{2,1,0:T(8,128)(2,1)} %spread_sum.1), calls=%async_computation.3 | async-start | bytes 655360 | tf_op jit(solution)/shard_map/all_to_all | solution.py:1197
  318.1 3.3 back_one.1
  324.5 4.0 %unpack_wide.1 = (f32[64,4608]{1,0:T(8,128)}, f32[64,4608]{1,0:T(8,128)}, f32[64,128]{1,0:T(8,128)}) custom-call(bf16[8,64,1152]{2,1,0:T(8,128)(2,1)} %copy-done.3, bf16[64,4608]{1,0:T(8,128)(2,1)} %gate_w.1, bf16[64,4608]{1,0:T(8,128)(2,1)} %up_w.1, f32[64,1]{1,0:T(8,128)} %copy.59.scale_ref), custom_call_target="tpu_custom_call" | custom-call | bytes 4751616 | tf_op jit(solution)/shard_map/unpack_wide/pallas_call | solution.py:42
  (270 shorter events, 107.8 us)
Async XLA Ops:
  7.2 95.1 %all-gather.6.cloned.1.call-start = ((), (), s32[]{:S(2)}) async-start(), calls=%async_computation.8 | async-start | bytes 3833856 | tf_op jit(solution)/shard_map/all_gather | solution.py:784
  24.0 12.7 %collective-permute-start.7 = (bf16[192,1024]{1,0:T(8,128)(2,1)S(1)}, bf16[192,1024]{1,0:T(8,128)(2,1)S(1)}, u32[]{:S(2)}, u32[]{:S(2)}) collective-permute-start(bf16[192,1024]{1,0:T(8,128)(2,1)S(1)} %fusion.1.refs_0_), channel_id=1, source_target_pairs={{0,5},{1,4},{2,7},{3,6},{4,1},{5,0},{6,3},{7,2},{8,13},{9,12},{10,... | collective-permute-start | bytes 1179656 | tf_op jit(solution)/shard_map/ppermute | solution.py:665
  26.0 38.4 %all-to-all-start = ((bf16[4,4,80,256]{3,2,1,0:T(8,128)(2,1)}), bf16[4,4,80,256]{3,2,1,0:T(8,128)(2,1)S(1)}, u32[]{:S(2)}, u32[]{:S(2)}) async-start(bf16[4,4,80,256]{3,2,1,0:T(8,128)(2,1)} %arrange_heads.1), calls=%async_computation | async-start | bytes 1310720 | tf_op jit(solution)/shard_map/all_to_all | solution.py:782
  30.8 113.1 %all-gather.4.cloned.1.call-start = ((), (), s32[]{:S(2)}) async-start(), calls=%async_computation.5 | async-start | bytes 5308416 | tf_op jit(solution)/shard_map/all_gather | solution.py:918
  30.8 14.3 %collective-permute-start.6 = (bf16[192,1024]{1,0:T(8,128)(2,1)S(1)}, bf16[192,1024]{1,0:T(8,128)(2,1)}, u32[]{:S(2)}, u32[]{:S(2)}) collective-permute-start(bf16[192,1024]{1,0:T(8,128)(2,1)S(1)} %fusion.1.refs_0_), channel_id=1, source_target_pairs={{0,4},{1,5},{2,6},{3,7},{4,0},{5,1},{6,2},{7,3},{8,12},{9,13},{10,... | collective-permute-start | bytes 1179656 | tf_op jit(solution)/shard_map/ppermute | solution.py:665
  32.1 13.6 %collective-permute-start.4 = (bf16[192,1024]{1,0:T(8,128)(2,1)S(1)}, bf16[192,1024]{1,0:T(8,128)(2,1)S(1)}, u32[]{:S(2)}, u32[]{:S(2)}) collective-permute-start(bf16[192,1024]{1,0:T(8,128)(2,1)S(1)} %fusion.1.refs_0_), channel_id=1, source_target_pairs={{0,2},{1,3},{2,0},{3,1},{4,6},{5,7},{6,4},{7,5},{8,10},{9,11},{10,... | collective-permute-start | bytes 1179656 | tf_op jit(solution)/shard_map/ppermute | solution.py:665
  32.1 15.5 %collective-permute-start.3 = (bf16[192,1024]{1,0:T(8,128)(2,1)S(1)}, bf16[192,1024]{1,0:T(8,128)(2,1)}, u32[]{:S(2)}, u32[]{:S(2)}) collective-permute-start(bf16[192,1024]{1,0:T(8,128)(2,1)S(1)} %fusion.1.refs_0_), channel_id=1, source_target_pairs={{0,1},{1,0},{2,3},{3,2},{4,5},{5,4},{6,7},{7,6},{8,9},{9,8},{10,11... | collective-permute-start | bytes 1179656 | tf_op jit(solution)/shard_map/ppermute | solution.py:665
  36.9 38.2 %collective-permute-start.12 = (bf16[192,1024]{1,0:T(8,128)(2,1)S(1)}, bf16[192,1024]{1,0:T(8,128)(2,1)S(1)}, u32[]{:S(2)}, u32[]{:S(2)}) collective-permute-start(bf16[192,1024]{1,0:T(8,128)(2,1)S(1)} %copy-done.31), channel_id=1, source_target_pairs={{0,5},{1,4},{2,7},{3,6},{4,1},{5,0},{6,3},{7,2},{8,13},{9,12},{10,... | collective-permute-start | bytes 1179656 | tf_op jit(solution)/shard_map/ppermute | solution.py:665
  45.2 29.9 %collective-permute-start.11 = (bf16[192,1024]{1,0:T(8,128)(2,1)S(1)}, bf16[192,1024]{1,0:T(8,128)(2,1)}, u32[]{:S(2)}, u32[]{:S(2)}) collective-permute-start(bf16[192,1024]{1,0:T(8,128)(2,1)S(1)} %copy-done.31), channel_id=1, source_target_pairs={{0,4},{1,5},{2,6},{3,7},{4,0},{5,1},{6,2},{7,3},{8,12},{9,13},{10,... | collective-permute-start | bytes 1179656 | tf_op jit(solution)/shard_map/ppermute | solution.py:665
  45.8 29.3 %collective-permute-start.10 = (bf16[192,1024]{1,0:T(8,128)(2,1)S(1)}, bf16[192,1024]{1,0:T(8,128)(2,1)}, u32[]{:S(2)}, u32[]{:S(2)}) collective-permute-start(bf16[192,1024]{1,0:T(8,128)(2,1)S(1)} %copy-done.31), channel_id=1, source_target_pairs={{0,1},{1,0},{2,3},{3,2},{4,5},{5,4},{6,7},{7,6},{8,9},{9,8},{10,11... | collective-permute-start | bytes 1179656 | tf_op jit(solution)/shard_map/ppermute | solution.py:665
  75.1 14.4 %collective-permute-start.13 = (bf16[1152,128]{1,0:T(8,128)(2,1)}, bf16[1152,128]{1,0:T(8,128)(2,1)S(1)}, u32[]{:S(2)}, u32[]{:S(2)}) collective-permute-start(bf16[1152,128]{1,0:T(8,128)(2,1)} %get-tuple-element.135), channel_id=1, source_target_pairs={{0,8},{8,16},{16,24},{1,9},{9,17},{17,25},{2,10},{10,18},{18,26},{... | collective-permute-start | bytes 884744 | tf_op jit(solution)/shard_map/ppermute | solution.py:889
  92.1 160.2 %reduce-scatter.3.cloned.1.call-start = ((), (), s32[]{:S(2)}) async-start(), calls=%async_computation.6 | async-start | bytes 5308416 | tf_op jit(solution)/shard_map/reduce_scatter | solution.py:1020
  117.0 18.8 %collective-permute-start.19 = (bf16[192,1024]{1,0:T(8,128)(2,1)}, bf16[192,1024]{1,0:T(8,128)(2,1)S(1)}, u32[]{:S(2)}, u32[]{:S(2)}) collective-permute-start(bf16[192,1024]{1,0:T(8,128)(2,1)} %get-tuple-element.148), channel_id=1, source_target_pairs={{0,4},{1,5},{2,6},{3,7},{4,0},{5,1},{6,2},{7,3},{8,12},{9,13},{10,... | collective-permute-start | bytes 1179656 | tf_op jit(solution)/shard_map/ppermute | solution.py:665
  118.4 18.5 %collective-permute-start.20 = (bf16[192,1024]{1,0:T(8,128)(2,1)}, bf16[192,1024]{1,0:T(8,128)(2,1)S(1)}, u32[]{:S(2)}, u32[]{:S(2)}) collective-permute-start(bf16[192,1024]{1,0:T(8,128)(2,1)} %get-tuple-element.149), channel_id=1, source_target_pairs={{0,5},{1,4},{2,7},{3,6},{4,1},{5,0},{6,3},{7,2},{8,13},{9,12},{10,... | collective-permute-start | bytes 1179656 | tf_op jit(solution)/shard_map/ppermute | solution.py:665
  140.5 13.2 %collective-permute-start.25 = (bf16[192,1024]{1,0:T(8,128)(2,1)}, bf16[192,1024]{1,0:T(8,128)(2,1)S(1)}, u32[]{:S(2)}, u32[]{:S(2)}) collective-permute-start(bf16[192,1024]{1,0:T(8,128)(2,1)} %get-tuple-element.151.refs_0_), channel_id=1, source_target_pairs={{0,4},{1,5},{2,6},{3,7},{4,0},{5,1},{6,2},{7,3},{8,12},{9,13},{10,... | collective-permute-start | bytes 1179656 | tf_op jit(solution)/shard_map/ppermute | solution.py:665
  142.9 27.8 %collective-permute-start.26 = (bf16[192,1024]{1,0:T(8,128)(2,1)}, bf16[192,1024]{1,0:T(8,128)(2,1)S(1)}, u32[]{:S(2)}, u32[]{:S(2)}) collective-permute-start(bf16[192,1024]{1,0:T(8,128)(2,1)} %get-tuple-element.151.refs_0_), channel_id=1, source_target_pairs={{0,5},{1,4},{2,7},{3,6},{4,1},{5,0},{6,3},{7,2},{8,13},{9,12},{10,... | collective-permute-start | bytes 1179656 | tf_op jit(solution)/shard_map/ppermute | solution.py:665
  168.6 24.5 %collective-permute-start.27 = (bf16[192,1024]{1,0:T(8,128)(2,1)}, bf16[192,1024]{1,0:T(8,128)(2,1)S(1)}, u32[]{:S(2)}, u32[]{:S(2)}) collective-permute-start(bf16[192,1024]{1,0:T(8,128)(2,1)} %get-tuple-element.175), channel_id=1, source_target_pairs={{0,1},{1,0},{2,3},{3,2},{4,5},{5,4},{6,7},{7,6},{8,9},{9,8},{10,11... | collective-permute-start | bytes 1179656 | tf_op jit(solution)/shard_map/ppermute | solution.py:665
  169.7 23.4 %collective-permute-start.28 = (bf16[192,1024]{1,0:T(8,128)(2,1)}, bf16[192,1024]{1,0:T(8,128)(2,1)S(1)}, u32[]{:S(2)}, u32[]{:S(2)}) collective-permute-start(bf16[192,1024]{1,0:T(8,128)(2,1)} %get-tuple-element.176), channel_id=1, source_target_pairs={{0,4},{1,5},{2,6},{3,7},{4,0},{5,1},{6,2},{7,3},{8,12},{9,13},{10,... | collective-permute-start | bytes 1179656 | tf_op jit(solution)/shard_map/ppermute | solution.py:665
  197.3 105.1 %reduce-scatter.5.cloned.1.call-start = ((), (), s32[]{:S(2)}) async-start(), calls=%async_computation.7 | async-start | bytes 3833856 | tf_op jit(solution)/shard_map/reduce_scatter | solution.py:1050
  198.3 13.0 %collective-permute-start.32 = (bf16[192,1024]{1,0:T(8,128)(2,1)S(1)}, bf16[192,1024]{1,0:T(8,128)(2,1)S(1)}, u32[]{:S(2)}, u32[]{:S(2)}) collective-permute-start(bf16[192,1024]{1,0:T(8,128)(2,1)S(1)} %copy-done.9), channel_id=1, source_target_pairs={{0,5},{1,4},{2,7},{3,6},{4,1},{5,0},{6,3},{7,2},{8,13},{9,12},{10,... | collective-permute-start | bytes 1179656 | tf_op jit(solution)/shard_map/ppermute | solution.py:665
  199.8 17.3 %collective-permute-start.31 = (bf16[192,1024]{1,0:T(8,128)(2,1)S(1)}, bf16[192,1024]{1,0:T(8,128)(2,1)S(1)}, u32[]{:S(2)}, u32[]{:S(2)}) collective-permute-start(bf16[192,1024]{1,0:T(8,128)(2,1)S(1)} %copy-done.9), channel_id=1, source_target_pairs={{0,4},{1,5},{2,6},{3,7},{4,0},{5,1},{6,2},{7,3},{8,12},{9,13},{10,... | collective-permute-start | bytes 1179656 | tf_op jit(solution)/shard_map/ppermute | solution.py:665
  200.8 16.5 %collective-permute-start.30 = (bf16[192,1024]{1,0:T(8,128)(2,1)S(1)}, bf16[192,1024]{1,0:T(8,128)(2,1)S(1)}, u32[]{:S(2)}, u32[]{:S(2)}) collective-permute-start(bf16[192,1024]{1,0:T(8,128)(2,1)S(1)} %copy-done.9), channel_id=1, source_target_pairs={{0,1},{1,0},{2,3},{3,2},{4,5},{5,4},{6,7},{7,6},{8,9},{9,8},{10,11... | collective-permute-start | bytes 1179656 | tf_op jit(solution)/shard_map/ppermute | solution.py:665
  243.6 26.7 %collective-permute-start.37 = (bf16[192,1024]{1,0:T(8,128)(2,1)S(1)}, bf16[192,1024]{1,0:T(8,128)(2,1)S(1)}, u32[]{:S(2)}, u32[]{:S(2)}) collective-permute-start(bf16[192,1024]{1,0:T(8,128)(2,1)S(1)} %copy-done.53), channel_id=1, source_target_pairs={{0,1},{1,0},{2,3},{3,2},{4,5},{5,4},{6,7},{7,6},{8,9},{9,8},{10,11... | collective-permute-start | bytes 1179656 | tf_op jit(solution)/shard_map/ppermute | solution.py:665
  245.1 26.4 %collective-permute-start.38 = (bf16[192,1024]{1,0:T(8,128)(2,1)S(1)}, bf16[192,1024]{1,0:T(8,128)(2,1)S(1)}, u32[]{:S(2)}, u32[]{:S(2)}) collective-permute-start(bf16[192,1024]{1,0:T(8,128)(2,1)S(1)} %copy-done.52), channel_id=1, source_target_pairs={{0,4},{1,5},{2,6},{3,7},{4,0},{5,1},{6,2},{7,3},{8,12},{9,13},{10,... | collective-permute-start | bytes 1179656 | tf_op jit(solution)/shard_map/ppermute | solution.py:665
  247.4 29.1 %collective-permute-start.39 = (bf16[192,1024]{1,0:T(8,128)(2,1)}, bf16[192,1024]{1,0:T(8,128)(2,1)}, u32[]{:S(2)}, u32[]{:S(2)}) collective-permute-start(bf16[192,1024]{1,0:T(8,128)(2,1)} %get-tuple-element.191), channel_id=1, source_target_pairs={{0,5},{1,4},{2,7},{3,6},{4,1},{5,0},{6,3},{7,2},{8,13},{9,12},{10,... | collective-permute-start | bytes 1179656 | tf_op jit(solution)/shard_map/ppermute | solution.py:665
  254.5 56.7 %all-to-all-start.1 = ((bf16[8,64,1152]{2,1,0:T(8,128)(2,1)}), bf16[8,64,1152]{2,1,0:T(8,128)(2,1)S(1)}, u32[]{:S(2)}, u32[]{:S(2)}) async-start(bf16[8,64,1152]{2,1,0:T(8,128)(2,1)} %bitcast.20), calls=%async_computation.2 | async-start | bytes 2359296 | tf_op jit(solution)/shard_map/all_to_all | solution.py:1090
  283.8 30.0 %collective-permute-start.45 = (bf16[192,1024]{1,0:T(8,128)(2,1)}, bf16[192,1024]{1,0:T(8,128)(2,1)S(1)}, u32[]{:S(2)}, u32[]{:S(2)}) collective-permute-start(bf16[192,1024]{1,0:T(8,128)(2,1)} %get-tuple-element.218), channel_id=1, source_target_pairs={{0,1},{1,0},{2,3},{3,2},{4,5},{5,4},{6,7},{7,6},{8,9},{9,8},{10,11... | collective-permute-start | bytes 1179656 | tf_op jit(solution)/shard_map/ppermute | solution.py:665
  285.2 28.6 %collective-permute-start.46 = (bf16[192,1024]{1,0:T(8,128)(2,1)}, bf16[192,1024]{1,0:T(8,128)(2,1)S(1)}, u32[]{:S(2)}, u32[]{:S(2)}) collective-permute-start(bf16[192,1024]{1,0:T(8,128)(2,1)} %get-tuple-element.219), channel_id=1, source_target_pairs={{0,4},{1,5},{2,6},{3,7},{4,0},{5,1},{6,2},{7,3},{8,12},{9,13},{10,... | collective-permute-start | bytes 1179656 | tf_op jit(solution)/shard_map/ppermute | solution.py:665
  286.7 27.1 %collective-permute-start.47 = (bf16[192,1024]{1,0:T(8,128)(2,1)}, bf16[192,1024]{1,0:T(8,128)(2,1)S(1)}, u32[]{:S(2)}, u32[]{:S(2)}) collective-permute-start(bf16[192,1024]{1,0:T(8,128)(2,1)} %get-tuple-element.220), channel_id=1, source_target_pairs={{0,5},{1,4},{2,7},{3,6},{4,1},{5,0},{6,3},{7,2},{8,13},{9,12},{10,... | collective-permute-start | bytes 1179656 | tf_op jit(solution)/shard_map/ppermute | solution.py:665
  287.3 16.6 %collective-permute-start.49 = (bf16[4,80,256]{2,1,0:T(8,128)(2,1)S(1)}, bf16[4,80,256]{2,1,0:T(8,128)(2,1)S(1)}, u32[]{:S(2)}, u32[]{:S(2)}) collective-permute-start(bf16[4,80,256]{2,1,0:T(8,128)(2,1)S(1)} %copy-done.58), channel_id=1, source_target_pairs={{0,16},{8,24},{16,0},{24,8},{1,17},{9,25},{17,1},{25,9},{2,18},{10... | collective-permute-start | bytes 491528 | tf_op jit(solution)/shard_map/ppermute | solution.py:661
  302.4 19.0 %collective-permute-start.51 = (bf16[208,1024]{1,0:T(8,128)(2,1)}, bf16[208,1024]{1,0:T(8,128)(2,1)S(1)}, u32[]{:S(2)}, u32[]{:S(2)}) collective-permute-start(bf16[208,1024]{1,0:T(8,128)(2,1)} %reduce-scatter.5.cloned.1.call-done.mine_ref), channel_id=1, source_target_pairs={{0,1},{1,0},{2,3},{3,2},{4,5},{5,4},{6,7},{7,6},{8,9},{9,8},{10,11... | collective-permute-start | bytes 1277960 | tf_op jit(solution)/shard_map/ppermute | solution.py:665
  314.6 15.3 %all-to-all-start.2 = ((bf16[8,80,256]{2,1,0:T(8,128)(2,1)}), bf16[8,80,256]{2,1,0:T(8,128)(2,1)S(1)}, u32[]{:S(2)}, u32[]{:S(2)}) async-start(bf16[8,80,256]{2,1,0:T(8,128)(2,1)} %spread_sum.1), calls=%async_computation.3 | async-start | bytes 655360 | tf_op jit(solution)/shard_map/all_to_all | solution.py:1197
  (90 other events, 528.4 us)
Sparse Core Ops, SparseCore 0:
  10.1 57.1 all-gather.5
  92.2 51.1 all-gather.3
  197.4 54.7 reduce-scatter.2
  254.4 47.9 reduce-scatter.4

commit v2 on v1

--- a/solution.py
+++ b/solution.py
@@ -1048,14 +1048,6 @@
         )(meta, *m_blocks, w_out, attended, grad_rest)
         grad_rest = grad_rest.reshape(-1, width)
         grad_rest = lax.psum_scatter(grad_rest, chips, scatter_dimension=0, tiled=True)
-        grad_down, grad_output = call(
-            rest_out_kernel,
-            [shape((seq * ff_rows, width), F32), shape((o_rows, width), F32)],
-            1,
-            [meta, grad_rest, swap(grad_rest, 1)],
-            0,
-            "rest_out",
-        )
     else:
         m_blocks = gather_blocks(d_mid)
         grad_gu = jnp.stack([tn(h_all, dgu_all[n]).astype(BF16) for n in range(2)])
@@ -1194,6 +1186,15 @@
             "spread_sum",
         )
         total = after(total, near_h[1:])
+        grad_rest = after(grad_rest, total)
+        grad_down, grad_output = call(
+            rest_out_kernel,
+            [shape((seq * ff_rows, width), F32), shape((o_rows, width), F32)],
+            1,
+            [meta, grad_rest, swap(grad_rest, 1)],
+            0,
+            "rest_out",
+        )
         owned = lax.all_to_all(total, ("a", "b", "c"), split_axis=0, concat_axis=0, tiled=True)
     else:
         owned = to_owners(lax.psum_scatter(grad_p[0], "o", scatter_dimension=0, tiled=True))

time: 344 us -> 342 us (level)
  Pallas kernels: 146 us -> 142 us
    reduce_scatter x1, waiting for transfers between devices: 13.2 us -> 0.01 us  [on_device(): lax.psum_scatter(grad_rest, chips, scatter_dimension=0, tiled=True)]
    ppermute x3, waiting for transfers between devices: 7.21 us -> 16 us  [outer_swap(): return lax.ppermute(value, 'o', [(r, r ^ mask) for r in range(count)])]
    pallas_call x2, Pallas kernels: 24.8 us -> 21.2 us  [attention(): pl.pallas_call(functools.partial(kernel, halo, span), grid=(steps,), in_s...]
    unnamed x126 -> x128, local copies, waits for them, and re-layouts: 15.2 us -> 14.2 us
  transfers between devices with their start and end apart: 59 -> 59, of which waited for: 25 -> 26; matrix products, arithmetic and copies ran while one was open for 4% -> 5% of each run, Pallas kernels for 41% -> 40%
where the time goes in v2:
time: 342 us; the launch traced here: 340 us
  Pallas kernels  142 us (42%)
  waiting for transfers between devices  91.3 us (27%)
  starting transfers between devices  58.9 us (17%)
  local copies, waits for them, and re-layouts  27 us (8%)
  between operations  14.4 us (4%)
  other arithmetic  6.79 us (2%)
    pallas_call x19, Pallas kernels, call(): pl.pallas_call(kernel, out_shape=outs, in_specs=[SM if n < n_smem else FA...  80.6 us
    ppermute x41, waiting for transfers between devices, swap(): lax.ppermute(value, ('a', 'b', 'c'), [(r, r ^ mask) for r in range(GROUP)])  42.9 us
    ppermute x41, starting transfers between devices, swap(): lax.ppermute(value, ('a', 'b', 'c'), [(r, r ^ mask) for r in range(GROUP)])  35.1 us
    pallas_call x3, Pallas kernels, feed(): pl.pallas_call(functools.partial(feed_kernel, count, down_rows), grid=(1,...  33 us
    pallas_call x2, Pallas kernels, attention(): pl.pallas_call(functools.partial(kernel, halo, span), grid=(steps,), in_s...  21.2 us
    ppermute x3, waiting for transfers between devices, outer_swap(): return lax.ppermute(value, 'o', [(r, r ^ mask) for r in range(count)])  16 us
    unnamed x128, local copies, waits for them, and re-layouts  14.2 us
    all_to_all x1, waiting for transfers between devices, on_device(): lax.all_to_all(packed, 'o', split_axis=0, concat_axis=0, tiled=True)  12.9 us
  transfers between devices with their start and end apart: 59, of which 26 were waited for; matrix products, arithmetic and copies ran while one was open for 5% of the time, Pallas kernels for 40%

profile of v2, /device:TPU:0, one launch (start us, length us, event | category | flops | bytes accessed | tf_op | source)
XLA Modules:
  0.0 340.3 jit_solution(5220753256577333445)
XLA Ops:
  26.0 4.9 %all-to-all-start = ((bf16[4,4,80,256]{3,2,1,0:T(8,128)(2,1)}), bf16[4,4,80,256]{3,2,1,0:T(8,128)(2,1)S(1)}, u32[]{:S(2)}, u32[]{:S(2)}) async-start(bf16[4,4,80,256]{3,2,1,0:T(8,128)(2,1)} %arrange_heads.1), calls=%async_computation | async-start | bytes 1310720 | tf_op jit(solution)/shard_map/all_to_all | solution.py:782
  32.7 4.0 %collective-permute-done.7.refs_5_ = bf16[192,1024]{1,0:T(8,128)(2,1)S(1)} collective-permute-done((bf16[192,1024]{1,0:T(8,128)(2,1)S(1)}, bf16[192,1024]{1,0:T(8,128)(2,1)S(1)}, u32[]{:S(2)}, u32[]{:S(2)}) %collective-permute-start.7) | collective-permute-done | bytes 393248 | tf_op jit(solution)/shard_map/ppermute | solution.py:665
  38.9 6.3 %collective-permute-done.6.refs_4_ = bf16[192,1024]{1,0:T(8,128)(2,1)} collective-permute-done((bf16[192,1024]{1,0:T(8,128)(2,1)S(1)}, bf16[192,1024]{1,0:T(8,128)(2,1)}, u32[]{:S(2)}, u32[]{:S(2)}) %collective-permute-start.6) | collective-permute-done | bytes 393248 | tf_op jit(solution)/shard_map/ppermute | solution.py:665
  51.4 12.9 %all-to-all-done = bf16[4,4,80,256]{3,2,1,0:T(8,128)(2,1)S(1)} async-done(((bf16[4,4,80,256]{3,2,1,0:T(8,128)(2,1)}), bf16[4,4,80,256]{3,2,1,0:T(8,128)(2,1)S(1)}, u32[]{:S(2)}, u32[]{:S(2)}) %all-to-all-start) | async-done | bytes 655392 | tf_op jit(solution)/shard_map/all_to_all | solution.py:782
  65.2 9.8 %prepare.1 = (bf16[2,1536,128]{2,1,0:T(8,128)(2,1)}, bf16[1536,128]{1,0:T(8,128)(2,1)}, bf16[1152,128]{1,0:T(8,128)(2,1)}, f32[1536,256]{1,0:T(8,128)}, bf16[153...) custom-call(s32[6]{0:T(128)} %stack.27.meta, bf16[192,1024]{1,0:T(8,128)(2,1)} %copy-done.6, ...), custom_call_target="tpu_custom_call" | custom-call | flops 805306368 | bytes 12099608 | tf_op jit(solution)/shard_map/prepare/pallas_call | solution.py:42
  77.1 3.1 send_wide.1
  82.0 5.0 %collective-permute-done.22.refs_2_ = bf16[64,1152]{1,0:T(8,128)(2,1)S(1)} collective-permute-done((bf16[64,1152]{1,0:T(8,128)(2,1)}, bf16[64,1152]{1,0:T(8,128)(2,1)S(1)}, u32[]{:S(2)}, u32[]{:S(2)}) %collective-permute-start.22) | collective-permute-done | bytes 147488 | tf_op jit(solution)/shard_map/ppermute | solution.py:657
  92.4 8.5 %attend.1 = (bf16[1536,128]{1,0:T(8,128)(2,1)}, f32[32,768]{1,0:T(8,128)}) custom-call(s32[6]{0:T(128)} %stack.27.meta, s32[10]{0:T(128)} %lengths.3, bf16[2,1536,128]{2,1,0:T(8,128)(2,1)} %get-tuple-element.133.q_ref, bf16[1152,128]{1,0:T(8,128)(2,1)} %copy-done.56, bf16[1536,128]{1,0:T(8,128)(2,1)} %get-tuple-element.137.refs_1_), custom_call_target="tpu_custom_call" | custom-call | flops 754974720 | bytes 2752512 | tf_op jit(solution)/shard_map/attend/pallas_call | solution.py:926
  102.9 3.9 %project.1 = (bf16[192,1024]{1,0:T(8,128)(2,1)}, bf16[192,1024]{1,0:T(8,128)(2,1)}, bf16[192,1024]{1,0:T(8,128)(2,1)}, bf16[192,1024]{1,0:T(8,128)(2,1)}, bf16[1...) custom-call(s32[6]{0:T(128)} %stack.27.meta, ...), custom_call_target="tpu_custom_call" | custom-call | flops 402653184 | bytes 3801112 | tf_op jit(solution)/shard_map/project/pallas_call | solution.py:42
  111.3 3.3 near.2
  118.1 8.7 %collective-permute-done.18.refs_2_ = bf16[192,1024]{1,0:T(8,128)(2,1)S(1)} collective-permute-done((bf16[192,1024]{1,0:T(8,128)(2,1)}, bf16[192,1024]{1,0:T(8,128)(2,1)S(1)}, u32[]{:S(2)}, u32[]{:S(2)}) %collective-permute-start.18) | collective-permute-done | bytes 393248 | tf_op jit(solution)/shard_map/ppermute | solution.py:665
  126.7 7.7 %collective-permute-done.19.refs_3_ = bf16[192,1024]{1,0:T(8,128)(2,1)S(1)} collective-permute-done((bf16[192,1024]{1,0:T(8,128)(2,1)}, bf16[192,1024]{1,0:T(8,128)(2,1)S(1)}, u32[]{:S(2)}, u32[]{:S(2)}) %collective-permute-start.19) | collective-permute-done | bytes 393248 | tf_op jit(solution)/shard_map/ppermute | solution.py:665
  143.4 9.6 %feed.3 = (bf16[192,1024]{1,0:T(8,128)(2,1)}, bf16[192,1024]{1,0:T(8,128)(2,1)}, bf16[768,1024]{1,0:T(8,128)(2,1)}, bf16[768,1024]{1,0:T(8,128)(2,1)}, bf16[2,76...) custom-call(bf16[192,1024]{1,0:T(8,128)(2,1)} %get-tuple-element.152.refs_0_, bf16[192,1024]{1,0:T(8,128)(2,1)} %refs_1_.2, ...), custom_call_target="tpu_custom_call" | custom-call | flops 2717908992 | bytes 11796480 | tf_op jit(solution)/shard_map/feed/pallas_call | solution.py:625
  154.0 13.7 %feed.4 = (bf16[192,1024]{1,0:T(8,128)(2,1)}, bf16[192,1024]{1,0:T(8,128)(2,1)}, bf16[192,1024]{1,0:T(8,128)(2,1)}, bf16[192,1024]{1,0:T(8,128)(2,1)}, bf16[768,...) custom-call(bf16[192,1024]{1,0:T(8,128)(2,1)} %copy-done.55, ...), custom_call_target="tpu_custom_call", output_to_operand_aliasing={{4}: (6, {}), {5}: (7, {}), {6}: (8, {}), {7}: (9, {})} | custom-call | flops 5435817984 | bytes 16515072 | tf_op jit(solution)/shard_map/feed/pallas_call | solution.py:625
  171.4 9.7 %feed.5 = (bf16[192,1024]{1,0:T(8,128)(2,1)}, bf16[192,1024]{1,0:T(8,128)(2,1)}, bf16[768,1024]{1,0:T(8,128)(2,1)}, bf16[768,1024]{1,0:T(8,128)(2,1)}, bf16[2,76...) custom-call(bf16[192,1024]{1,0:T(8,128)(2,1)} %copy-done.41, ...), custom_call_target="tpu_custom_call", output_to_operand_aliasing={{2}: (4, {}), {3}: (5, {}), {4}: (6, {}), {5}: (7, {})} | custom-call | flops 2717908992 | bytes 11796480 | tf_op jit(solution)/shard_map/feed/pallas_call | solution.py:625
  181.7 10.4 %wide_grad.1 = bf16[4,2,256,1152]{3,2,1,0:T(8,128)(2,1)} custom-call(bf16[768,1024]{1,0:T(8,128)(2,1)} %get-tuple-element.223.h_ref, bf16[2,768,1152]{2,1,0:T(8,128)(2,1)} %get-tuple-element.224.d_ref), custom_call_target="tpu_custom_call" | custom-call | bytes 9830400 | tf_op jit(solution)/shard_map/wide_grad/pallas_call | solution.py:42
  193.7 3.2 back_two.1
  201.4 6.4 %down_grad.1.refs_10_ = bf16[4,2,208,1024]{3,2,1,0:T(8,128)(2,1)} custom-call(bf16[2,768,640]{2,1,0:T(8,128)(2,1)} %get-tuple-element.180.inner_ref, bf16[768,1024]{1,0:T(8,128)(2,1)} %get-tuple-element.181.c_ref), custom_call_target="tpu_custom_call" | custom-call | bytes 6946816 | tf_op jit(solution)/shard_map/down_grad/pallas_call | solution.py:42
  207.8 3.1 collective-permute-done.32.refs_5_
  210.9 6.2 %collective-permute-done.31.refs_4_ = bf16[192,1024]{1,0:T(8,128)(2,1)S(1)} collective-permute-done((bf16[192,1024]{1,0:T(8,128)(2,1)S(1)}, bf16[192,1024]{1,0:T(8,128)(2,1)S(1)}, u32[]{:S(2)}, u32[]{:S(2)}) %collective-permute-start.31) | collective-permute-done | bytes 393248 | tf_op jit(solution)/shard_map/ppermute | solution.py:665
  221.5 7.1 %unproject.1 = (bf16[1536,128]{1,0:T(8,128)(2,1)}, bf16[4,2,208,1024]{3,2,1,0:T(8,128)(2,1)}) custom-call(s32[6]{0:T(128)} %stack.27.meta, bf16[192,1024]{1,0:T(8,128)(2,1)} %get-tuple-element.182.refs_0_, bf16[192,1024]{1,0:T(8,128)(2,1)} %copy-done.12, bf16[192,1024]{1,0:T(8,128)(2,1)} %copy-done.13, ...), custom_call_target="tpu_custom_call", output_to_operand_aliasing={{1}: (11, {})} | custom-call | flops 805306368 | bytes 8388608 | tf_op jit(solution)/shard_map/unproject/pallas_call | solution.py:1031
  228.7 12.7 %attend_back.1 = (bf16[1536,128]{1,0:T(8,128)(2,1)}, bf16[1152,128]{1,0:T(8,128)(2,1)}, f32[1536,128]{1,0:T(8,128)}) custom-call(s32[6]{0:T(128)} %stack.27.meta, s32[10]{0:T(128)} %lengths.3, bf16[2,1536,128]{2,1,0:T(8,128)(2,1)} %get-tuple-element.133.q_ref, bf16[1152,128]{1,0:T(8,128)(2,1)} %copy-done.56, bf16[1536,128]{1,0:T(8,128)(2,1)} %get-tuple-element.137.refs_1_, ...), custom_call_target="tpu_custom_call" | custom-call | flops 2264924160 | bytes 2752512 | tf_op jit(solution)/shard_map/attend_back/pallas_call | solution.py:926
  246.3 5.9 %reduce-scatter.3.cloned.1.call-done = bf16[256,1152]{1,0:T(8,128)(2,1)} async-done(((bf16[2048,1152]{1,0:T(8,128)(2,1)}), bf16[256,1152]{1,0:T(8,128)(2,1)}) %reduce-scatter.3.cloned.1.call-update) | async-done | bytes 589840 | tf_op jit(solution)/shard_map/reduce_scatter | solution.py:1020
  254.4 3.6 %all-to-all-start.1 = ((bf16[8,64,1152]{2,1,0:T(8,128)(2,1)}), bf16[8,64,1152]{2,1,0:T(8,128)(2,1)S(1)}, u32[]{:S(2)}, u32[]{:S(2)}) async-start(bf16[8,64,1152]{2,1,0:T(8,128)(2,1)} %bitcast.20), calls=%async_computation.2 | async-start | bytes 2359296 | tf_op jit(solution)/shard_map/all_to_all | solution.py:1082
  260.2 10.8 %finish.1 = (bf16[192,1024]{1,0:T(8,128)(2,1)}, bf16[192,1024]{1,0:T(8,128)(2,1)}, bf16[192,1024]{1,0:T(8,128)(2,1)}, bf16[192,1024]{1,0:T(8,128)(2,1)}, bf16[19...) custom-call(s32[6]{0:T(128)} %stack.27.meta, ...), custom_call_target="tpu_custom_call" | custom-call | flops 805306368 | bytes 9093144 | tf_op jit(solution)/shard_map/finish/pallas_call | solution.py:42
  273.6 4.2 %project_grad.1 = (bf16[4,80,256]{2,1,0:T(8,128)(2,1)}, bf16[4,80,256]{2,1,0:T(8,128)(2,1)}, bf16[4,80,256]{2,1,0:T(8,128)(2,1)}, bf16[4,80,256]{2,1,0:T(8,128)(2,1)}) custom-call(s32[6]{0:T(128)} %stack.27.meta, bf16[1536,1024]{1,0:T(8,128)(2,1)} %get-tuple-element.207.n_ref, bf16[1536,256]{1,0:T(8,128)(2,1)} %get-tuple-element.208.d_ref, ...), custom_call_target="tpu_custom_call" | custom-call | flops 805306368 | bytes 4595736 | tf_op jit(solution)/shard_map/project_grad/pallas_call | solution.py:42
  281.3 3.2 near.3
  290.0 10.0 %collective-permute-done.48.refs_1_ = bf16[4,80,256]{2,1,0:T(8,128)(2,1)S(1)} collective-permute-done((bf16[4,80,256]{2,1,0:T(8,128)(2,1)S(1)}, bf16[4,80,256]{2,1,0:T(8,128)(2,1)S(1)}, u32[]{:S(2)}, u32[]{:S(2)}) %collective-permute-start.48) | collective-permute-done | bytes 163872 | tf_op jit(solution)/shard_map/ppermute | solution.py:661
  301.8 6.0 %collective-permute-done.50.refs_3_ = bf16[4,80,256]{2,1,0:T(8,128)(2,1)S(1)} collective-permute-done((bf16[4,80,256]{2,1,0:T(8,128)(2,1)S(1)}, bf16[4,80,256]{2,1,0:T(8,128)(2,1)S(1)}, u32[]{:S(2)}, u32[]{:S(2)}) %collective-permute-start.50) | collective-permute-done | bytes 163872 | tf_op jit(solution)/shard_map/ppermute | solution.py:661
  310.4 3.7 %all-to-all-start.2 = ((bf16[8,80,256]{2,1,0:T(8,128)(2,1)}), bf16[8,80,256]{2,1,0:T(8,128)(2,1)S(1)}, u32[]{:S(2)}, u32[]{:S(2)}) async-start(bf16[8,80,256]{2,1,0:T(8,128)(2,1)} %spread_sum.1), calls=%async_computation.3 | async-start | bytes 655360 | tf_op jit(solution)/shard_map/all_to_all | solution.py:1198
  314.2 3.3 back_one.1
  319.6 4.0 %unpack_wide.1 = (f32[64,4608]{1,0:T(8,128)}, f32[64,4608]{1,0:T(8,128)}, f32[64,128]{1,0:T(8,128)}) custom-call(bf16[8,64,1152]{2,1,0:T(8,128)(2,1)} %copy-done.3, bf16[64,4608]{1,0:T(8,128)(2,1)} %gate_w.1, bf16[64,4608]{1,0:T(8,128)(2,1)} %up_w.1, f32[64,1]{1,0:T(8,128)} %copy.59.scale_ref), custom_call_target="tpu_custom_call" | custom-call | bytes 4751616 | tf_op jit(solution)/shard_map/unpack_wide/pallas_call | solution.py:42
  (272 shorter events, 111.1 us)
Async XLA Ops:
  7.2 93.7 %all-gather.6.cloned.1.call-start = ((), (), s32[]{:S(2)}) async-start(), calls=%async_computation.8 | async-start | bytes 3833856 | tf_op jit(solution)/shard_map/all_gather | solution.py:784
  24.0 12.7 %collective-permute-start.7 = (bf16[192,1024]{1,0:T(8,128)(2,1)S(1)}, bf16[192,1024]{1,0:T(8,128)(2,1)S(1)}, u32[]{:S(2)}, u32[]{:S(2)}) collective-permute-start(bf16[192,1024]{1,0:T(8,128)(2,1)S(1)} %fusion.1.refs_0_), channel_id=1, source_target_pairs={{0,5},{1,4},{2,7},{3,6},{4,1},{5,0},{6,3},{7,2},{8,13},{9,12},{10,... | collective-permute-start | bytes 1179656 | tf_op jit(solution)/shard_map/ppermute | solution.py:665
  26.0 38.4 %all-to-all-start = ((bf16[4,4,80,256]{3,2,1,0:T(8,128)(2,1)}), bf16[4,4,80,256]{3,2,1,0:T(8,128)(2,1)S(1)}, u32[]{:S(2)}, u32[]{:S(2)}) async-start(bf16[4,4,80,256]{3,2,1,0:T(8,128)(2,1)} %arrange_heads.1), calls=%async_computation | async-start | bytes 1310720 | tf_op jit(solution)/shard_map/all_to_all | solution.py:782
  30.8 112.6 %all-gather.4.cloned.1.call-start = ((), (), s32[]{:S(2)}) async-start(), calls=%async_computation.5 | async-start | bytes 5308416 | tf_op jit(solution)/shard_map/all_gather | solution.py:918
  30.8 14.3 %collective-permute-start.6 = (bf16[192,1024]{1,0:T(8,128)(2,1)S(1)}, bf16[192,1024]{1,0:T(8,128)(2,1)}, u32[]{:S(2)}, u32[]{:S(2)}) collective-permute-start(bf16[192,1024]{1,0:T(8,128)(2,1)S(1)} %fusion.1.refs_0_), channel_id=1, source_target_pairs={{0,4},{1,5},{2,6},{3,7},{4,0},{5,1},{6,2},{7,3},{8,12},{9,13},{10,... | collective-permute-start | bytes 1179656 | tf_op jit(solution)/shard_map/ppermute | solution.py:665
  32.1 13.6 %collective-permute-start.4 = (bf16[192,1024]{1,0:T(8,128)(2,1)S(1)}, bf16[192,1024]{1,0:T(8,128)(2,1)S(1)}, u32[]{:S(2)}, u32[]{:S(2)}) collective-permute-start(bf16[192,1024]{1,0:T(8,128)(2,1)S(1)} %fusion.1.refs_0_), channel_id=1, source_target_pairs={{0,2},{1,3},{2,0},{3,1},{4,6},{5,7},{6,4},{7,5},{8,10},{9,11},{10,... | collective-permute-start | bytes 1179656 | tf_op jit(solution)/shard_map/ppermute | solution.py:665
  32.1 15.5 %collective-permute-start.3 = (bf16[192,1024]{1,0:T(8,128)(2,1)S(1)}, bf16[192,1024]{1,0:T(8,128)(2,1)}, u32[]{:S(2)}, u32[]{:S(2)}) collective-permute-start(bf16[192,1024]{1,0:T(8,128)(2,1)S(1)} %fusion.1.refs_0_), channel_id=1, source_target_pairs={{0,1},{1,0},{2,3},{3,2},{4,5},{5,4},{6,7},{7,6},{8,9},{9,8},{10,11... | collective-permute-start | bytes 1179656 | tf_op jit(solution)/shard_map/ppermute | solution.py:665
  36.9 38.2 %collective-permute-start.12 = (bf16[192,1024]{1,0:T(8,128)(2,1)S(1)}, bf16[192,1024]{1,0:T(8,128)(2,1)S(1)}, u32[]{:S(2)}, u32[]{:S(2)}) collective-permute-start(bf16[192,1024]{1,0:T(8,128)(2,1)S(1)} %copy-done.31), channel_id=1, source_target_pairs={{0,5},{1,4},{2,7},{3,6},{4,1},{5,0},{6,3},{7,2},{8,13},{9,12},{10,... | collective-permute-start | bytes 1179656 | tf_op jit(solution)/shard_map/ppermute | solution.py:665
  45.1 29.9 %collective-permute-start.11 = (bf16[192,1024]{1,0:T(8,128)(2,1)S(1)}, bf16[192,1024]{1,0:T(8,128)(2,1)}, u32[]{:S(2)}, u32[]{:S(2)}) collective-permute-start(bf16[192,1024]{1,0:T(8,128)(2,1)S(1)} %copy-done.31), channel_id=1, source_target_pairs={{0,4},{1,5},{2,6},{3,7},{4,0},{5,1},{6,2},{7,3},{8,12},{9,13},{10,... | collective-permute-start | bytes 1179656 | tf_op jit(solution)/shard_map/ppermute | solution.py:665
  45.8 29.3 %collective-permute-start.10 = (bf16[192,1024]{1,0:T(8,128)(2,1)S(1)}, bf16[192,1024]{1,0:T(8,128)(2,1)}, u32[]{:S(2)}, u32[]{:S(2)}) collective-permute-start(bf16[192,1024]{1,0:T(8,128)(2,1)S(1)} %copy-done.31), channel_id=1, source_target_pairs={{0,1},{1,0},{2,3},{3,2},{4,5},{5,4},{6,7},{7,6},{8,9},{9,8},{10,11... | collective-permute-start | bytes 1179656 | tf_op jit(solution)/shard_map/ppermute | solution.py:665
  75.0 14.4 %collective-permute-start.13 = (bf16[1152,128]{1,0:T(8,128)(2,1)}, bf16[1152,128]{1,0:T(8,128)(2,1)S(1)}, u32[]{:S(2)}, u32[]{:S(2)}) collective-permute-start(bf16[1152,128]{1,0:T(8,128)(2,1)} %get-tuple-element.136), channel_id=1, source_target_pairs={{0,8},{8,16},{16,24},{1,9},{9,17},{17,25},{2,10},{10,18},{18,26},{... | collective-permute-start | bytes 884744 | tf_op jit(solution)/shard_map/ppermute | solution.py:889
  92.1 160.1 %reduce-scatter.3.cloned.1.call-start = ((), (), s32[]{:S(2)}) async-start(), calls=%async_computation.6 | async-start | bytes 5308416 | tf_op jit(solution)/shard_map/reduce_scatter | solution.py:1020
  115.8 18.6 %collective-permute-start.19 = (bf16[192,1024]{1,0:T(8,128)(2,1)}, bf16[192,1024]{1,0:T(8,128)(2,1)S(1)}, u32[]{:S(2)}, u32[]{:S(2)}) collective-permute-start(bf16[192,1024]{1,0:T(8,128)(2,1)} %get-tuple-element.149), channel_id=1, source_target_pairs={{0,4},{1,5},{2,6},{3,7},{4,0},{5,1},{6,2},{7,3},{8,12},{9,13},{10,... | collective-permute-start | bytes 1179656 | tf_op jit(solution)/shard_map/ppermute | solution.py:665
  117.2 18.2 %collective-permute-start.20 = (bf16[192,1024]{1,0:T(8,128)(2,1)}, bf16[192,1024]{1,0:T(8,128)(2,1)S(1)}, u32[]{:S(2)}, u32[]{:S(2)}) collective-permute-start(bf16[192,1024]{1,0:T(8,128)(2,1)} %get-tuple-element.150), channel_id=1, source_target_pairs={{0,5},{1,4},{2,7},{3,6},{4,1},{5,0},{6,3},{7,2},{8,13},{9,12},{10,... | collective-permute-start | bytes 1179656 | tf_op jit(solution)/shard_map/ppermute | solution.py:665
  139.0 14.1 %collective-permute-start.25 = (bf16[192,1024]{1,0:T(8,128)(2,1)}, bf16[192,1024]{1,0:T(8,128)(2,1)S(1)}, u32[]{:S(2)}, u32[]{:S(2)}) collective-permute-start(bf16[192,1024]{1,0:T(8,128)(2,1)} %get-tuple-element.152.refs_0_), channel_id=1, source_target_pairs={{0,4},{1,5},{2,6},{3,7},{4,0},{5,1},{6,2},{7,3},{8,12},{9,13},{10,... | collective-permute-start | bytes 1179656 | tf_op jit(solution)/shard_map/ppermute | solution.py:665
  141.5 29.2 %collective-permute-start.26 = (bf16[192,1024]{1,0:T(8,128)(2,1)}, bf16[192,1024]{1,0:T(8,128)(2,1)S(1)}, u32[]{:S(2)}, u32[]{:S(2)}) collective-permute-start(bf16[192,1024]{1,0:T(8,128)(2,1)} %get-tuple-element.152.refs_0_), channel_id=1, source_target_pairs={{0,5},{1,4},{2,7},{3,6},{4,1},{5,0},{6,3},{7,2},{8,13},{9,12},{10,... | collective-permute-start | bytes 1179656 | tf_op jit(solution)/shard_map/ppermute | solution.py:665
  167.6 24.5 %collective-permute-start.27 = (bf16[192,1024]{1,0:T(8,128)(2,1)}, bf16[192,1024]{1,0:T(8,128)(2,1)S(1)}, u32[]{:S(2)}, u32[]{:S(2)}) collective-permute-start(bf16[192,1024]{1,0:T(8,128)(2,1)} %get-tuple-element.176), channel_id=1, source_target_pairs={{0,1},{1,0},{2,3},{3,2},{4,5},{5,4},{6,7},{7,6},{8,9},{9,8},{10,11... | collective-permute-start | bytes 1179656 | tf_op jit(solution)/shard_map/ppermute | solution.py:665
  169.2 23.0 %collective-permute-start.28 = (bf16[192,1024]{1,0:T(8,128)(2,1)}, bf16[192,1024]{1,0:T(8,128)(2,1)S(1)}, u32[]{:S(2)}, u32[]{:S(2)}) collective-permute-start(bf16[192,1024]{1,0:T(8,128)(2,1)} %get-tuple-element.177), channel_id=1, source_target_pairs={{0,4},{1,5},{2,6},{3,7},{4,0},{5,1},{6,2},{7,3},{8,12},{9,13},{10,... | collective-permute-start | bytes 1179656 | tf_op jit(solution)/shard_map/ppermute | solution.py:665
  196.9 120.6 %reduce-scatter.5.cloned.1.call-start = ((), (), s32[]{:S(2)}) async-start(), calls=%async_computation.7 | async-start | bytes 3833856 | tf_op jit(solution)/shard_map/reduce_scatter | solution.py:1050
  197.9 13.0 %collective-permute-start.32 = (bf16[192,1024]{1,0:T(8,128)(2,1)S(1)}, bf16[192,1024]{1,0:T(8,128)(2,1)S(1)}, u32[]{:S(2)}, u32[]{:S(2)}) collective-permute-start(bf16[192,1024]{1,0:T(8,128)(2,1)S(1)} %copy-done.9), channel_id=1, source_target_pairs={{0,5},{1,4},{2,7},{3,6},{4,1},{5,0},{6,3},{7,2},{8,13},{9,12},{10,... | collective-permute-start | bytes 1179656 | tf_op jit(solution)/shard_map/ppermute | solution.py:665
  199.7 17.4 %collective-permute-start.31 = (bf16[192,1024]{1,0:T(8,128)(2,1)S(1)}, bf16[192,1024]{1,0:T(8,128)(2,1)S(1)}, u32[]{:S(2)}, u32[]{:S(2)}) collective-permute-start(bf16[192,1024]{1,0:T(8,128)(2,1)S(1)} %copy-done.9), channel_id=1, source_target_pairs={{0,4},{1,5},{2,6},{3,7},{4,0},{5,1},{6,2},{7,3},{8,12},{9,13},{10,... | collective-permute-start | bytes 1179656 | tf_op jit(solution)/shard_map/ppermute | solution.py:665
  200.3 16.9 %collective-permute-start.30 = (bf16[192,1024]{1,0:T(8,128)(2,1)S(1)}, bf16[192,1024]{1,0:T(8,128)(2,1)S(1)}, u32[]{:S(2)}, u32[]{:S(2)}) collective-permute-start(bf16[192,1024]{1,0:T(8,128)(2,1)S(1)} %copy-done.9), channel_id=1, source_target_pairs={{0,1},{1,0},{2,3},{3,2},{4,5},{5,4},{6,7},{7,6},{8,9},{9,8},{10,11... | collective-permute-start | bytes 1179656 | tf_op jit(solution)/shard_map/ppermute | solution.py:665
  241.4 30.2 %collective-permute-start.37 = (bf16[192,1024]{1,0:T(8,128)(2,1)S(1)}, bf16[192,1024]{1,0:T(8,128)(2,1)S(1)}, u32[]{:S(2)}, u32[]{:S(2)}) collective-permute-start(bf16[192,1024]{1,0:T(8,128)(2,1)S(1)} %copy-done.53), channel_id=1, source_target_pairs={{0,1},{1,0},{2,3},{3,2},{4,5},{5,4},{6,7},{7,6},{8,9},{9,8},{10,11... | collective-permute-start | bytes 1179656 | tf_op jit(solution)/shard_map/ppermute | solution.py:665
  242.9 29.5 %collective-permute-start.38 = (bf16[192,1024]{1,0:T(8,128)(2,1)S(1)}, bf16[192,1024]{1,0:T(8,128)(2,1)S(1)}, u32[]{:S(2)}, u32[]{:S(2)}) collective-permute-start(bf16[192,1024]{1,0:T(8,128)(2,1)S(1)} %copy-done.52), channel_id=1, source_target_pairs={{0,4},{1,5},{2,6},{3,7},{4,0},{5,1},{6,2},{7,3},{8,12},{9,13},{10,... | collective-permute-start | bytes 1179656 | tf_op jit(solution)/shard_map/ppermute | solution.py:665
  243.9 15.6 %collective-permute-start.40 = (bf16[1152,128]{1,0:T(8,128)(2,1)}, bf16[1152,128]{1,0:T(8,128)(2,1)S(1)}, u32[]{:S(2)}, u32[]{:S(2)}) collective-permute-start(bf16[1152,128]{1,0:T(8,128)(2,1)} %get-tuple-element.195), channel_id=1, source_target_pairs={{8,0},{16,8},{24,16},{9,1},{17,9},{25,17},{10,2},{18,10},{26,18},{... | collective-permute-start | bytes 884744 | tf_op jit(solution)/shard_map/ppermute | solution.py:1113
  245.2 32.6 %collective-permute-start.39 = (bf16[192,1024]{1,0:T(8,128)(2,1)}, bf16[192,1024]{1,0:T(8,128)(2,1)}, u32[]{:S(2)}, u32[]{:S(2)}) collective-permute-start(bf16[192,1024]{1,0:T(8,128)(2,1)} %get-tuple-element.192), channel_id=1, source_target_pairs={{0,5},{1,4},{2,7},{3,6},{4,1},{5,0},{6,3},{7,2},{8,13},{9,12},{10,... | collective-permute-start | bytes 1179656 | tf_op jit(solution)/shard_map/ppermute | solution.py:665
  254.4 53.4 %all-to-all-start.1 = ((bf16[8,64,1152]{2,1,0:T(8,128)(2,1)}), bf16[8,64,1152]{2,1,0:T(8,128)(2,1)S(1)}, u32[]{:S(2)}, u32[]{:S(2)}) async-start(bf16[8,64,1152]{2,1,0:T(8,128)(2,1)} %bitcast.20), calls=%async_computation.2 | async-start | bytes 2359296 | tf_op jit(solution)/shard_map/all_to_all | solution.py:1082
  284.5 25.9 %collective-permute-start.45 = (bf16[192,1024]{1,0:T(8,128)(2,1)}, bf16[192,1024]{1,0:T(8,128)(2,1)S(1)}, u32[]{:S(2)}, u32[]{:S(2)}) collective-permute-start(bf16[192,1024]{1,0:T(8,128)(2,1)} %get-tuple-element.219), channel_id=1, source_target_pairs={{0,1},{1,0},{2,3},{3,2},{4,5},{5,4},{6,7},{7,6},{8,9},{9,8},{10,11... | collective-permute-start | bytes 1179656 | tf_op jit(solution)/shard_map/ppermute | solution.py:665
  285.4 25.0 %collective-permute-start.46 = (bf16[192,1024]{1,0:T(8,128)(2,1)}, bf16[192,1024]{1,0:T(8,128)(2,1)S(1)}, u32[]{:S(2)}, u32[]{:S(2)}) collective-permute-start(bf16[192,1024]{1,0:T(8,128)(2,1)} %get-tuple-element.220), channel_id=1, source_target_pairs={{0,4},{1,5},{2,6},{3,7},{4,0},{5,1},{6,2},{7,3},{8,12},{9,13},{10,... | collective-permute-start | bytes 1179656 | tf_op jit(solution)/shard_map/ppermute | solution.py:665
  286.6 23.8 %collective-permute-start.47 = (bf16[192,1024]{1,0:T(8,128)(2,1)}, bf16[192,1024]{1,0:T(8,128)(2,1)S(1)}, u32[]{:S(2)}, u32[]{:S(2)}) collective-permute-start(bf16[192,1024]{1,0:T(8,128)(2,1)} %get-tuple-element.221), channel_id=1, source_target_pairs={{0,5},{1,4},{2,7},{3,6},{4,1},{5,0},{6,3},{7,2},{8,13},{9,12},{10,... | collective-permute-start | bytes 1179656 | tf_op jit(solution)/shard_map/ppermute | solution.py:665
  310.4 14.5 %all-to-all-start.2 = ((bf16[8,80,256]{2,1,0:T(8,128)(2,1)}), bf16[8,80,256]{2,1,0:T(8,128)(2,1)S(1)}, u32[]{:S(2)}, u32[]{:S(2)}) async-start(bf16[8,80,256]{2,1,0:T(8,128)(2,1)} %spread_sum.1), calls=%async_computation.3 | async-start | bytes 655360 | tf_op jit(solution)/shard_map/all_to_all | solution.py:1198
  317.5 13.2 %collective-permute-start.51 = (bf16[208,1024]{1,0:T(8,128)(2,1)}, bf16[208,1024]{1,0:T(8,128)(2,1)S(1)}, u32[]{:S(2)}, u32[]{:S(2)}) collective-permute-start(bf16[208,1024]{1,0:T(8,128)(2,1)} %reduce-scatter.5.cloned.1.call-done.mine_ref), channel_id=1, source_target_pairs={{0,1},{1,0},{2,3},{3,2},{4,5},{5,4},{6,7},{7,6},{8,9},{9,8},{10,11... | collective-permute-start | bytes 1277960 | tf_op jit(solution)/shard_map/ppermute | solution.py:665
  (91 other events, 513.4 us)
Sparse Core Ops, SparseCore 0:
  10.1 57.1 all-gather.5
  92.2 51.1 all-gather.3
  197.0 55.0 reduce-scatter.2
  254.3 43.0 reduce-scatter.4
